TPU v7x, 512 devices: a whole 4x8x8 slice. The times are simulated.
512 devices in a mesh: cuts: 16 (over z_lo, x, core), space: 32 (over z_hi, y).
Axes of the slice: x: 4, y: 8, z: 8 (z_hi: 4, z_lo: 2; z = z_hi * 2 + z_lo), core: 2. Of those that a mesh axis runs over, the one named last changes fastest.
Arguments:
- start_u: float32 [16, 256, 32, 128], P('cuts', 'space'), may hold values from 0.4 to 1
- start_v: float32 [16, 256, 32, 128], P('cuts', 'space'), may hold values from 0 to 0.5
Outputs:
- next_u: float32 [16, 256, 32, 128], P('cuts', 'space')
- next_v: float32 [16, 256, 32, 128], P('cuts', 'space')
All inputs are finite; a program needn't handle non-finite values.
Results may differ from a plain program's by a relative error of at most 0.00002.
Values sent between devices are 32-bit elements; how exact they have to be, the bound alone decides.
A program may use at most 64 MiB of HBM per device.

v0:
```python
import jax
import jax.numpy as jnp
from jax import lax
from jax.sharding import PartitionSpec as P

GZ = 128
COARSEN = 2
FINE_STEPS = 4
COARSE_STEPS = 2


SPREAD_FIRST = 0.14
SPREAD_SECOND = 0.13
FEED_RATE = 0.035
KILL_RATE = 0.065
COARSE_DT = 2.0


def with_halo(block, sides, width):
    for axis, dim in sides:
        count = lax.axis_size(axis)
        forward = [(i, i + 1) for i in range(count - 1)]
        forward.append((count - 1, 0))
        backward = [(target, source) for source, target in forward]
        low = lax.ppermute(
            lax.slice_in_dim(block, block.shape[dim] - width, None, axis=dim), axis, forward
        )
        high = lax.ppermute(lax.slice_in_dim(block, 0, width, axis=dim), axis, backward)
        block = jnp.concatenate([low, block, high], axis=dim)
    return block


def joined_along(blocks, dim):
    lengths = list(blocks.shape[1:])
    lengths[dim] *= blocks.shape[0]
    return jnp.moveaxis(blocks, 0, dim).reshape(lengths)


def sent_to_all(array, axis):
    copies = jnp.broadcast_to(array, (lax.axis_size(axis), *array.shape))
    return lax.all_to_all(copies, axis, split_axis=0, concat_axis=0, tiled=True)


def collect(array, axis, dim):
    return joined_along(sent_to_all(array, axis), dim)


def broadcast(array, axis, root):
    return lax.dynamic_index_in_dim(lax.all_gather(array, axis), root, 0, keepdims=False)


def reaction(fields, laplace, step_size):
    first = fields[0]
    second = fields[1]
    feeding = first * second * second
    new_first = first + step_size * (
        SPREAD_FIRST * laplace[0] - feeding + FEED_RATE * (1.0 - first)
    )
    new_second = second + step_size * (
        SPREAD_SECOND * laplace[1] + feeding - (FEED_RATE + KILL_RATE) * second
    )
    return jnp.stack([new_first, new_second], axis=0)


def fine_update(padded):
    inner = padded[:, 1:-1]
    beside_all = padded[:, 2:] + padded[:, :-2]
    beside_all = beside_all + jnp.roll(inner, 1, 2) + jnp.roll(inner, -1, 2)
    beside_all = beside_all + jnp.roll(inner, 1, 3) + jnp.roll(inner, -1, 3)
    return reaction(inner, beside_all - 6.0 * inner, 1.0)


def coarse_laplace(fields, width):
    places = lax.broadcasted_iota(jnp.int32, fields.shape, 2) % width
    beside_all = jnp.roll(fields, 1, 1) + jnp.roll(fields, -1, 1)
    beside_all = beside_all + jnp.roll(fields, width, 2) + jnp.roll(fields, -width, 2)
    upper = jnp.where(places == width - 1, jnp.roll(fields, width - 1, 2), jnp.roll(fields, -1, 2))
    lower = jnp.where(places == 0, jnp.roll(fields, 1 - width, 2), jnp.roll(fields, 1, 2))
    return beside_all + upper + lower - 6.0 * fields


def march_whole(fields):
    width = GZ // COARSEN
    factor = 1.0 / (COARSEN * COARSEN)
    for sweep in range(COARSE_STEPS):
        fields = reaction(fields, coarse_laplace(fields, width) * factor, COARSE_DT)
    return fields


def march_padded(padded):
    fields = march_whole(padded)
    return fields[:, COARSE_STEPS : fields.shape[1] - COARSE_STEPS]


def restrict_flat(fields):
    extent = fields.shape
    blocks = fields.reshape(
        2,
        extent[1] // COARSEN,
        COARSEN,
        extent[2] // COARSEN,
        COARSEN,
        extent[3] // COARSEN,
        COARSEN,
    )
    means = jnp.mean(blocks, axis=(2, 4, 6))
    return means.reshape(2, extent[1] // COARSEN, extent[2] // COARSEN * (extent[3] // COARSEN))


def on_device(start_u, start_v):
    fields = jnp.stack([start_u[0], start_v[0]], axis=0)
    finals = with_halo(fields, (("space", 1),), FINE_STEPS)
    for sweep in range(FINE_STEPS):
        finals = fine_update(finals)
    start_piece = restrict_flat(fields)
    end_piece = restrict_flat(finals)
    start_padded = with_halo(start_piece, (("space", 1),), COARSE_STEPS)
    correction = end_piece - march_padded(start_padded)
    cut_index = lax.axis_index("cuts")
    cut_count = lax.axis_size("cuts")
    rows = start_piece.shape[1]
    every_term = collect(correction[None], "cuts", 0)
    current = broadcast(start_piece, "cuts", 0)

    def local_link(position, carry):
        state, kept = carry
        padded = with_halo(state, (("space", 1),), COARSE_STEPS)
        state = march_padded(padded) + every_term[position]
        kept = jnp.where(cut_index == position, state, kept)
        return (state, kept)

    final_state, mine = lax.fori_loop(0, cut_count, local_link, (current, correction))
    own_coarse = mine - end_piece
    extent = finals.shape
    own_coarse = own_coarse.reshape(2, rows, extent[2] // COARSEN, extent[3] // COARSEN)
    spread = jnp.repeat(own_coarse, COARSEN, axis=1)
    spread = jnp.repeat(spread, COARSEN, axis=2)
    spread = jnp.repeat(spread, COARSEN, axis=3)
    results = finals + spread
    return (results[0][None], results[1][None])


def solution(mesh):
    return jax.shard_map(
        on_device,
        mesh=mesh,
        in_specs=(P("cuts", "space", None, None), P("cuts", "space", None, None)),
        out_specs=(P("cuts", "space", None, None), P("cuts", "space", None, None)),
        check_vma=False,
    )
```

profile of v0, /device:TPU:64, one launch (start us, length us, event | category | flops | bytes accessed | tf_op | source)
XLA Modules:
  0.0 345.1 jit_solution(9667261952699862745)
XLA Ops:
  1.5 0.9 constant_dynamic-update-slice_fusion
  2.5 18.1 %reshape.45 = f32[2,4,2,16,2,64,2]{6,5,4,3,2,1,0:T(8,128)} reshape(f32[2,8,32,128]{3,2,1,0:T(8,128)S(1)} %constant_dynamic-update-slice_fusion) | data formatting | bytes 524288 | tf_op jit(solution)/shard_map/reshape | solution.py:97
  20.6 7.0 %reduce_sum.18 = f32[2,4,16,64]{3,2,1,0:T(8,128)S(1)} reduce(f32[2,4,2,16,2,64,2]{6,5,4,3,2,1,0:T(8,128)} %reshape.45, f32[]{:T(128)} %constant.209.clone.1), dimensions={2,4,6}, to_apply=%region_0.1 | reduce | flops 57344 | bytes 294916 | tf_op jit(solution)/shard_map/reduce_sum | solution.py:106
  27.7 3.5 %collective-permute-start.4 = (f32[2,2,1024]{2,1,0:T(2,128)S(1)}, f32[2,2,1024]{2,1,0:T(2,128)S(1)}, u32[]{:S(2)}, u32[]{:S(2)}) collective-permute-start(f32[2,2,1024]{2,1,0:T(2,128)S(1)} %get-tuple-element.268), channel_id=1, source_target_pairs={{0,1},{1,2},{2,3},{3,4},{4,5},{5,6},{6,7},{7,8},{8,9},{9,10},{10,1... | collective-permute-start | bytes 49160 | tf_op jit(solution)/shard_map/ppermute | solution.py:25
  31.2 11.4 %collective-permute-start.5 = (f32[2,2,1024]{2,1,0:T(2,128)S(1)}, f32[2,2,1024]{2,1,0:T(2,128)S(1)}, u32[]{:S(2)}, u32[]{:S(2)}) collective-permute-start(f32[2,2,1024]{2,1,0:T(2,128)S(1)} %get-tuple-element.269), channel_id=1, source_target_pairs={{1,0},{2,1},{3,2},{4,3},{5,4},{6,5},{7,6},{8,7},{9,8},{10,9},{11,1... | collective-permute-start | bytes 49160 | tf_op jit(solution)/shard_map/ppermute | solution.py:28
  42.6 1.9 collective-permute-start.2
  44.5 8.1 %collective-permute-start.3 = (f32[2,4,32,128]{3,2,1,0:T(8,128)S(1)}, f32[2,4,32,128]{3,2,1,0:T(8,128)S(1)}, u32[]{:S(2)}, u32[]{:S(2)}) collective-permute-start(f32[2,4,32,128]{3,2,1,0:T(8,128)S(1)} %get-tuple-element.233), channel_id=1, source_target_pairs={{1,0},{2,1},{3,2},{4,3},{5,4},{6,5},{7,6},{8,7},{9,8},{10,9},{11,1... | collective-permute-start | bytes 393224 | tf_op jit(solution)/shard_map/ppermute | solution.py:28
  54.1 1.9 collective-permute-done.2
  59.6 9.8 %stack.76 = f32[1,4,2,16,2,64,2]{6,5,4,3,2,1,0:T(8,128)} reshape(f32[1,8,32,128]{3,2,1,0:T(8,128)S(1)} %get-tuple-element.200) | data formatting | bytes 262144 | tf_op jit(solution)/shard_map/stack | solution.py:62
  69.4 5.4 %copy.21 = f32[1,4,2,16,2,64,2]{5,3,6,4,2,1,0:T(8,128)S(1)} copy(f32[1,4,2,16,2,64,2]{6,5,4,3,2,1,0:T(8,128)} %stack.76) | data formatting | bytes 262144 | tf_op jit(solution)/shard_map/stack | solution.py:62
  74.8 9.8 %stack.77 = f32[1,4,2,16,2,64,2]{6,5,4,3,2,1,0:T(8,128)} reshape(f32[1,8,32,128]{3,2,1,0:T(8,128)S(1)} %get-tuple-element.201) | data formatting | bytes 262144 | tf_op jit(solution)/shard_map/stack | solution.py:62
  84.6 5.4 %copy.22 = f32[1,4,2,16,2,64,2]{5,3,6,4,2,1,0:T(8,128)S(1)} copy(f32[1,4,2,16,2,64,2]{6,5,4,3,2,1,0:T(8,128)} %stack.77) | data formatting | bytes 262144 | tf_op jit(solution)/shard_map/stack | solution.py:62
  90.2 0.9 broadcast_in_dim.13
  91.2 5.8 %all-to-all-start = ((f32[16,1,2,4,1024]{4,3,2,1,0:T(4,128)}), f32[16,1,2,4,1024]{4,3,2,1,0:T(4,128)S(1)}, u32[]{:S(2)}, u32[]{:S(2)}) async-start(f32[16,1,2,4,1024]{4,3,2,1,0:T(4,128)} %broadcast_in_dim.13), calls=%async_computation | async-start | bytes 1048576 | tf_op jit(solution)/shard_map/all_to_all | solution.py:41
  97.0 22.7 %all_gather.3 = f32[16,2,4,1024]{3,2,1,0:T(4,128)S(1)} all-gather(f32[1,2,4,1024]{3,2,1,0:T(4,128)S(1)} %div.13), channel_id=1, replica_groups=mesh['cuts'=16,'space'=32] {'cuts'}, dimensions={0}, use_global_device_ids=true | all-gather | bytes 557056 | tf_op jit(solution)/shard_map/all_gather | solution.py:49
  120.2 222.4 %while.17 = (s32[]{:T(128)}, f32[2,4,1024]{2,1,0:T(4,128)S(1)}, f32[2,4,1024]{2,1,0:T(4,128)S(1)}, f32[16,2,4,1024]{3,2,1,0:T(4,128)S(1)}, s32[]{:T(128)}, /*index=5*/s32[]{:T(128)}) while((s32[]{:T(128)}, f32[2,4,1024]{2,1,0:T(4,128)S(1)}, f32[2,4,1024]{2,1,0:T(4,128)S(1)}, f32[16,2,4,1024]{3,2,1,0:T(4,128)S(1)}, s32[]{:T(128)}, ...), condition=%wide.region_3.4_spmd, body=%wide.region_2.3_spmd.sunk | while | flops 1177603 | bytes 4353195 | solution.py:132
  120.2 9.3 %collective-permute-start = (f32[2,2,1024]{2,1,0:T(2,128)S(1)}, f32[2,2,1024]{2,1,0:T(2,128)S(1)}, u32[]{:S(2)}, u32[]{:S(2)}) collective-permute-start(f32[2,2,1024]{2,1,0:T(2,128)S(1)} %get-tuple-element.343), channel_id=1, source_target_pairs={{1,0},{2,1},{3,2},{4,3},{5,4},{6,5},{7,6},{8,7},{9,8},{10,9},{11,1... | collective-permute-start | bytes 49160 | tf_op jit(solution)/shard_map/while/body/eval_jaxpr/ppermute | solution.py:28
  129.6 1.9 collective-permute-start.1
  131.5 8.1 %collective-permute-done.1 = f32[2,2,1024]{2,1,0:T(2,128)S(1)} collective-permute-done((f32[2,2,1024]{2,1,0:T(2,128)S(1)}, f32[2,2,1024]{2,1,0:T(2,128)S(1)}, u32[]{:S(2)}, u32[]{:S(2)}) %collective-permute-start.1) | collective-permute-done | bytes 16416 | tf_op jit(solution)/shard_map/while/body/eval_jaxpr/ppermute | solution.py:25
  141.1 1.9 collective-permute-start
  143.0 3.9 %collective-permute-start.1 = (f32[2,2,1024]{2,1,0:T(2,128)S(1)}, f32[2,2,1024]{2,1,0:T(2,128)S(1)}, u32[]{:S(2)}, u32[]{:S(2)}) collective-permute-start(f32[2,2,1024]{2,1,0:T(2,128)S(1)} %get-tuple-element.344), channel_id=1, source_target_pairs={{0,1},{1,2},{2,3},{3,4},{4,5},{5,6},{6,7},{7,8},{8,9},{9,10},{10,1... | collective-permute-start | bytes 49160 | tf_op jit(solution)/shard_map/while/body/eval_jaxpr/ppermute | solution.py:25
  147.0 6.0 %collective-permute-done.1 = f32[2,2,1024]{2,1,0:T(2,128)S(1)} collective-permute-done((f32[2,2,1024]{2,1,0:T(2,128)S(1)}, f32[2,2,1024]{2,1,0:T(2,128)S(1)}, u32[]{:S(2)}, u32[]{:S(2)}) %collective-permute-start.1) | collective-permute-done | bytes 16416 | tf_op jit(solution)/shard_map/while/body/eval_jaxpr/ppermute | solution.py:25
  154.5 1.9 collective-permute-start
  156.4 3.9 %collective-permute-start.1 = (f32[2,2,1024]{2,1,0:T(2,128)S(1)}, f32[2,2,1024]{2,1,0:T(2,128)S(1)}, u32[]{:S(2)}, u32[]{:S(2)}) collective-permute-start(f32[2,2,1024]{2,1,0:T(2,128)S(1)} %get-tuple-element.344), channel_id=1, source_target_pairs={{0,1},{1,2},{2,3},{3,4},{4,5},{5,6},{6,7},{7,8},{8,9},{9,10},{10,1... | collective-permute-start | bytes 49160 | tf_op jit(solution)/shard_map/while/body/eval_jaxpr/ppermute | solution.py:25
  160.4 6.0 %collective-permute-done.1 = f32[2,2,1024]{2,1,0:T(2,128)S(1)} collective-permute-done((f32[2,2,1024]{2,1,0:T(2,128)S(1)}, f32[2,2,1024]{2,1,0:T(2,128)S(1)}, u32[]{:S(2)}, u32[]{:S(2)}) %collective-permute-start.1) | collective-permute-done | bytes 16416 | tf_op jit(solution)/shard_map/while/body/eval_jaxpr/ppermute | solution.py:25
  168.0 1.9 collective-permute-start
  169.9 3.9 %collective-permute-start.1 = (f32[2,2,1024]{2,1,0:T(2,128)S(1)}, f32[2,2,1024]{2,1,0:T(2,128)S(1)}, u32[]{:S(2)}, u32[]{:S(2)}) collective-permute-start(f32[2,2,1024]{2,1,0:T(2,128)S(1)} %get-tuple-element.344), channel_id=1, source_target_pairs={{0,1},{1,2},{2,3},{3,4},{4,5},{5,6},{6,7},{7,8},{8,9},{9,10},{10,1... | collective-permute-start | bytes 49160 | tf_op jit(solution)/shard_map/while/body/eval_jaxpr/ppermute | solution.py:25
  173.8 6.1 %collective-permute-done.1 = f32[2,2,1024]{2,1,0:T(2,128)S(1)} collective-permute-done((f32[2,2,1024]{2,1,0:T(2,128)S(1)}, f32[2,2,1024]{2,1,0:T(2,128)S(1)}, u32[]{:S(2)}, u32[]{:S(2)}) %collective-permute-start.1) | collective-permute-done | bytes 16416 | tf_op jit(solution)/shard_map/while/body/eval_jaxpr/ppermute | solution.py:25
  181.4 1.9 collective-permute-start
  183.3 3.9 %collective-permute-start.1 = (f32[2,2,1024]{2,1,0:T(2,128)S(1)}, f32[2,2,1024]{2,1,0:T(2,128)S(1)}, u32[]{:S(2)}, u32[]{:S(2)}) collective-permute-start(f32[2,2,1024]{2,1,0:T(2,128)S(1)} %get-tuple-element.344), channel_id=1, source_target_pairs={{0,1},{1,2},{2,3},{3,4},{4,5},{5,6},{6,7},{7,8},{8,9},{9,10},{10,1... | collective-permute-start | bytes 49160 | tf_op jit(solution)/shard_map/while/body/eval_jaxpr/ppermute | solution.py:25
  187.3 6.1 %collective-permute-done.1 = f32[2,2,1024]{2,1,0:T(2,128)S(1)} collective-permute-done((f32[2,2,1024]{2,1,0:T(2,128)S(1)}, f32[2,2,1024]{2,1,0:T(2,128)S(1)}, u32[]{:S(2)}, u32[]{:S(2)}) %collective-permute-start.1) | collective-permute-done | bytes 16416 | tf_op jit(solution)/shard_map/while/body/eval_jaxpr/ppermute | solution.py:25
  194.9 1.9 collective-permute-start
  196.8 3.9 %collective-permute-start.1 = (f32[2,2,1024]{2,1,0:T(2,128)S(1)}, f32[2,2,1024]{2,1,0:T(2,128)S(1)}, u32[]{:S(2)}, u32[]{:S(2)}) collective-permute-start(f32[2,2,1024]{2,1,0:T(2,128)S(1)} %get-tuple-element.344), channel_id=1, source_target_pairs={{0,1},{1,2},{2,3},{3,4},{4,5},{5,6},{6,7},{7,8},{8,9},{9,10},{10,1... | collective-permute-start | bytes 49160 | tf_op jit(solution)/shard_map/while/body/eval_jaxpr/ppermute | solution.py:25
  200.8 6.1 %collective-permute-done.1 = f32[2,2,1024]{2,1,0:T(2,128)S(1)} collective-permute-done((f32[2,2,1024]{2,1,0:T(2,128)S(1)}, f32[2,2,1024]{2,1,0:T(2,128)S(1)}, u32[]{:S(2)}, u32[]{:S(2)}) %collective-permute-start.1) | collective-permute-done | bytes 16416 | tf_op jit(solution)/shard_map/while/body/eval_jaxpr/ppermute | solution.py:25
  208.3 1.9 collective-permute-start
  210.3 3.9 %collective-permute-start.1 = (f32[2,2,1024]{2,1,0:T(2,128)S(1)}, f32[2,2,1024]{2,1,0:T(2,128)S(1)}, u32[]{:S(2)}, u32[]{:S(2)}) collective-permute-start(f32[2,2,1024]{2,1,0:T(2,128)S(1)} %get-tuple-element.344), channel_id=1, source_target_pairs={{0,1},{1,2},{2,3},{3,4},{4,5},{5,6},{6,7},{7,8},{8,9},{9,10},{10,1... | collective-permute-start | bytes 49160 | tf_op jit(solution)/shard_map/while/body/eval_jaxpr/ppermute | solution.py:25
  214.2 6.0 %collective-permute-done.1 = f32[2,2,1024]{2,1,0:T(2,128)S(1)} collective-permute-done((f32[2,2,1024]{2,1,0:T(2,128)S(1)}, f32[2,2,1024]{2,1,0:T(2,128)S(1)}, u32[]{:S(2)}, u32[]{:S(2)}) %collective-permute-start.1) | collective-permute-done | bytes 16416 | tf_op jit(solution)/shard_map/while/body/eval_jaxpr/ppermute | solution.py:25
  221.8 1.9 collective-permute-start
  223.7 3.9 %collective-permute-start.1 = (f32[2,2,1024]{2,1,0:T(2,128)S(1)}, f32[2,2,1024]{2,1,0:T(2,128)S(1)}, u32[]{:S(2)}, u32[]{:S(2)}) collective-permute-start(f32[2,2,1024]{2,1,0:T(2,128)S(1)} %get-tuple-element.344), channel_id=1, source_target_pairs={{0,1},{1,2},{2,3},{3,4},{4,5},{5,6},{6,7},{7,8},{8,9},{9,10},{10,1... | collective-permute-start | bytes 49160 | tf_op jit(solution)/shard_map/while/body/eval_jaxpr/ppermute | solution.py:25
  227.7 6.0 %collective-permute-done.1 = f32[2,2,1024]{2,1,0:T(2,128)S(1)} collective-permute-done((f32[2,2,1024]{2,1,0:T(2,128)S(1)}, f32[2,2,1024]{2,1,0:T(2,128)S(1)}, u32[]{:S(2)}, u32[]{:S(2)}) %collective-permute-start.1) | collective-permute-done | bytes 16416 | tf_op jit(solution)/shard_map/while/body/eval_jaxpr/ppermute | solution.py:25
  235.2 1.9 collective-permute-start
  237.1 3.9 %collective-permute-start.1 = (f32[2,2,1024]{2,1,0:T(2,128)S(1)}, f32[2,2,1024]{2,1,0:T(2,128)S(1)}, u32[]{:S(2)}, u32[]{:S(2)}) collective-permute-start(f32[2,2,1024]{2,1,0:T(2,128)S(1)} %get-tuple-element.344), channel_id=1, source_target_pairs={{0,1},{1,2},{2,3},{3,4},{4,5},{5,6},{6,7},{7,8},{8,9},{9,10},{10,1... | collective-permute-start | bytes 49160 | tf_op jit(solution)/shard_map/while/body/eval_jaxpr/ppermute | solution.py:25
  241.1 6.0 %collective-permute-done.1 = f32[2,2,1024]{2,1,0:T(2,128)S(1)} collective-permute-done((f32[2,2,1024]{2,1,0:T(2,128)S(1)}, f32[2,2,1024]{2,1,0:T(2,128)S(1)}, u32[]{:S(2)}, u32[]{:S(2)}) %collective-permute-start.1) | collective-permute-done | bytes 16416 | tf_op jit(solution)/shard_map/while/body/eval_jaxpr/ppermute | solution.py:25
  248.7 1.9 collective-permute-start
  250.6 3.9 %collective-permute-start.1 = (f32[2,2,1024]{2,1,0:T(2,128)S(1)}, f32[2,2,1024]{2,1,0:T(2,128)S(1)}, u32[]{:S(2)}, u32[]{:S(2)}) collective-permute-start(f32[2,2,1024]{2,1,0:T(2,128)S(1)} %get-tuple-element.344), channel_id=1, source_target_pairs={{0,1},{1,2},{2,3},{3,4},{4,5},{5,6},{6,7},{7,8},{8,9},{9,10},{10,1... | collective-permute-start | bytes 49160 | tf_op jit(solution)/shard_map/while/body/eval_jaxpr/ppermute | solution.py:25
  254.6 6.0 %collective-permute-done.1 = f32[2,2,1024]{2,1,0:T(2,128)S(1)} collective-permute-done((f32[2,2,1024]{2,1,0:T(2,128)S(1)}, f32[2,2,1024]{2,1,0:T(2,128)S(1)}, u32[]{:S(2)}, u32[]{:S(2)}) %collective-permute-start.1) | collective-permute-done | bytes 16416 | tf_op jit(solution)/shard_map/while/body/eval_jaxpr/ppermute | solution.py:25
  262.1 1.9 collective-permute-start
  264.0 3.9 %collective-permute-start.1 = (f32[2,2,1024]{2,1,0:T(2,128)S(1)}, f32[2,2,1024]{2,1,0:T(2,128)S(1)}, u32[]{:S(2)}, u32[]{:S(2)}) collective-permute-start(f32[2,2,1024]{2,1,0:T(2,128)S(1)} %get-tuple-element.344), channel_id=1, source_target_pairs={{0,1},{1,2},{2,3},{3,4},{4,5},{5,6},{6,7},{7,8},{8,9},{9,10},{10,1... | collective-permute-start | bytes 49160 | tf_op jit(solution)/shard_map/while/body/eval_jaxpr/ppermute | solution.py:25
  268.0 6.1 %collective-permute-done.1 = f32[2,2,1024]{2,1,0:T(2,128)S(1)} collective-permute-done((f32[2,2,1024]{2,1,0:T(2,128)S(1)}, f32[2,2,1024]{2,1,0:T(2,128)S(1)}, u32[]{:S(2)}, u32[]{:S(2)}) %collective-permute-start.1) | collective-permute-done | bytes 16416 | tf_op jit(solution)/shard_map/while/body/eval_jaxpr/ppermute | solution.py:25
  275.5 1.9 collective-permute-start
  277.5 3.9 %collective-permute-start.1 = (f32[2,2,1024]{2,1,0:T(2,128)S(1)}, f32[2,2,1024]{2,1,0:T(2,128)S(1)}, u32[]{:S(2)}, u32[]{:S(2)}) collective-permute-start(f32[2,2,1024]{2,1,0:T(2,128)S(1)} %get-tuple-element.344), channel_id=1, source_target_pairs={{0,1},{1,2},{2,3},{3,4},{4,5},{5,6},{6,7},{7,8},{8,9},{9,10},{10,1... | collective-permute-start | bytes 49160 | tf_op jit(solution)/shard_map/while/body/eval_jaxpr/ppermute | solution.py:25
  281.4 6.0 %collective-permute-done.1 = f32[2,2,1024]{2,1,0:T(2,128)S(1)} collective-permute-done((f32[2,2,1024]{2,1,0:T(2,128)S(1)}, f32[2,2,1024]{2,1,0:T(2,128)S(1)}, u32[]{:S(2)}, u32[]{:S(2)}) %collective-permute-start.1) | collective-permute-done | bytes 16416 | tf_op jit(solution)/shard_map/while/body/eval_jaxpr/ppermute | solution.py:25
  289.0 1.9 collective-permute-start
  290.9 3.9 %collective-permute-start.1 = (f32[2,2,1024]{2,1,0:T(2,128)S(1)}, f32[2,2,1024]{2,1,0:T(2,128)S(1)}, u32[]{:S(2)}, u32[]{:S(2)}) collective-permute-start(f32[2,2,1024]{2,1,0:T(2,128)S(1)} %get-tuple-element.344), channel_id=1, source_target_pairs={{0,1},{1,2},{2,3},{3,4},{4,5},{5,6},{6,7},{7,8},{8,9},{9,10},{10,1... | collective-permute-start | bytes 49160 | tf_op jit(solution)/shard_map/while/body/eval_jaxpr/ppermute | solution.py:25
  294.9 6.0 %collective-permute-done.1 = f32[2,2,1024]{2,1,0:T(2,128)S(1)} collective-permute-done((f32[2,2,1024]{2,1,0:T(2,128)S(1)}, f32[2,2,1024]{2,1,0:T(2,128)S(1)}, u32[]{:S(2)}, u32[]{:S(2)}) %collective-permute-start.1) | collective-permute-done | bytes 16416 | tf_op jit(solution)/shard_map/while/body/eval_jaxpr/ppermute | solution.py:25
  302.4 1.9 collective-permute-start
  304.3 3.9 %collective-permute-start.1 = (f32[2,2,1024]{2,1,0:T(2,128)S(1)}, f32[2,2,1024]{2,1,0:T(2,128)S(1)}, u32[]{:S(2)}, u32[]{:S(2)}) collective-permute-start(f32[2,2,1024]{2,1,0:T(2,128)S(1)} %get-tuple-element.344), channel_id=1, source_target_pairs={{0,1},{1,2},{2,3},{3,4},{4,5},{5,6},{6,7},{7,8},{8,9},{9,10},{10,1... | collective-permute-start | bytes 49160 | tf_op jit(solution)/shard_map/while/body/eval_jaxpr/ppermute | solution.py:25
  308.3 6.0 %collective-permute-done.1 = f32[2,2,1024]{2,1,0:T(2,128)S(1)} collective-permute-done((f32[2,2,1024]{2,1,0:T(2,128)S(1)}, f32[2,2,1024]{2,1,0:T(2,128)S(1)}, u32[]{:S(2)}, u32[]{:S(2)}) %collective-permute-start.1) | collective-permute-done | bytes 16416 | tf_op jit(solution)/shard_map/while/body/eval_jaxpr/ppermute | solution.py:25
  315.8 1.9 collective-permute-start
  317.7 3.9 %collective-permute-start.1 = (f32[2,2,1024]{2,1,0:T(2,128)S(1)}, f32[2,2,1024]{2,1,0:T(2,128)S(1)}, u32[]{:S(2)}, u32[]{:S(2)}) collective-permute-start(f32[2,2,1024]{2,1,0:T(2,128)S(1)} %get-tuple-element.344), channel_id=1, source_target_pairs={{0,1},{1,2},{2,3},{3,4},{4,5},{5,6},{6,7},{7,8},{8,9},{9,10},{10,1... | collective-permute-start | bytes 49160 | tf_op jit(solution)/shard_map/while/body/eval_jaxpr/ppermute | solution.py:25
  321.7 6.0 %collective-permute-done.1 = f32[2,2,1024]{2,1,0:T(2,128)S(1)} collective-permute-done((f32[2,2,1024]{2,1,0:T(2,128)S(1)}, f32[2,2,1024]{2,1,0:T(2,128)S(1)}, u32[]{:S(2)}, u32[]{:S(2)}) %collective-permute-start.1) | collective-permute-done | bytes 16416 | tf_op jit(solution)/shard_map/while/body/eval_jaxpr/ppermute | solution.py:25
  329.2 1.9 collective-permute-start
  331.1 3.9 %collective-permute-start.1 = (f32[2,2,1024]{2,1,0:T(2,128)S(1)}, f32[2,2,1024]{2,1,0:T(2,128)S(1)}, u32[]{:S(2)}, u32[]{:S(2)}) collective-permute-start(f32[2,2,1024]{2,1,0:T(2,128)S(1)} %get-tuple-element.344), channel_id=1, source_target_pairs={{0,1},{1,2},{2,3},{3,4},{4,5},{5,6},{6,7},{7,8},{8,9},{9,10},{10,1... | collective-permute-start | bytes 49160 | tf_op jit(solution)/shard_map/while/body/eval_jaxpr/ppermute | solution.py:25
  335.1 6.0 %collective-permute-done.1 = f32[2,2,1024]{2,1,0:T(2,128)S(1)} collective-permute-done((f32[2,2,1024]{2,1,0:T(2,128)S(1)}, f32[2,2,1024]{2,1,0:T(2,128)S(1)}, u32[]{:S(2)}, u32[]{:S(2)}) %collective-permute-start.1) | collective-permute-done | bytes 16416 | tf_op jit(solution)/shard_map/while/body/eval_jaxpr/ppermute | solution.py:25
  (508 shorter events, 31.7 us)
Async XLA Ops:
  27.7 25.0 %collective-permute-start.4 = (f32[2,2,1024]{2,1,0:T(2,128)S(1)}, f32[2,2,1024]{2,1,0:T(2,128)S(1)}, u32[]{:S(2)}, u32[]{:S(2)}) collective-permute-start(f32[2,2,1024]{2,1,0:T(2,128)S(1)} %get-tuple-element.268), channel_id=1, source_target_pairs={{0,1},{1,2},{2,3},{3,4},{4,5},{5,6},{6,7},{7,8},{8,9},{9,10},{10,1... | collective-permute-start | bytes 49160 | tf_op jit(solution)/shard_map/ppermute | solution.py:25
  31.2 21.5 %collective-permute-start.5 = (f32[2,2,1024]{2,1,0:T(2,128)S(1)}, f32[2,2,1024]{2,1,0:T(2,128)S(1)}, u32[]{:S(2)}, u32[]{:S(2)}) collective-permute-start(f32[2,2,1024]{2,1,0:T(2,128)S(1)} %get-tuple-element.269), channel_id=1, source_target_pairs={{1,0},{2,1},{3,2},{4,3},{5,4},{6,5},{7,6},{8,7},{9,8},{10,9},{11,1... | collective-permute-start | bytes 49160 | tf_op jit(solution)/shard_map/ppermute | solution.py:28
  42.6 13.4 %collective-permute-start.2 = (f32[2,4,32,128]{3,2,1,0:T(8,128)S(1)}, f32[2,4,32,128]{3,2,1,0:T(8,128)S(1)}, u32[]{:S(2)}, u32[]{:S(2)}) collective-permute-start(f32[2,4,32,128]{3,2,1,0:T(8,128)S(1)} %get-tuple-element.232), channel_id=1, source_target_pairs={{0,1},{1,2},{2,3},{3,4},{4,5},{5,6},{6,7},{7,8},{8,9},{9,10},{10,1... | collective-permute-start | bytes 393224 | tf_op jit(solution)/shard_map/ppermute | solution.py:25
  44.5 11.5 %collective-permute-start.3 = (f32[2,4,32,128]{3,2,1,0:T(8,128)S(1)}, f32[2,4,32,128]{3,2,1,0:T(8,128)S(1)}, u32[]{:S(2)}, u32[]{:S(2)}) collective-permute-start(f32[2,4,32,128]{3,2,1,0:T(8,128)S(1)} %get-tuple-element.233), channel_id=1, source_target_pairs={{1,0},{2,1},{3,2},{4,3},{5,4},{6,5},{7,6},{8,7},{9,8},{10,9},{11,1... | collective-permute-start | bytes 393224 | tf_op jit(solution)/shard_map/ppermute | solution.py:28
  91.2 29.0 %all-to-all-start = ((f32[16,1,2,4,1024]{4,3,2,1,0:T(4,128)}), f32[16,1,2,4,1024]{4,3,2,1,0:T(4,128)S(1)}, u32[]{:S(2)}, u32[]{:S(2)}) async-start(f32[16,1,2,4,1024]{4,3,2,1,0:T(4,128)} %broadcast_in_dim.13), calls=%async_computation | async-start | bytes 1048576 | tf_op jit(solution)/shard_map/all_to_all | solution.py:41
  120.2 11.3 %collective-permute-start = (f32[2,2,1024]{2,1,0:T(2,128)S(1)}, f32[2,2,1024]{2,1,0:T(2,128)S(1)}, u32[]{:S(2)}, u32[]{:S(2)}) collective-permute-start(f32[2,2,1024]{2,1,0:T(2,128)S(1)} %get-tuple-element.343), channel_id=1, source_target_pairs={{1,0},{2,1},{3,2},{4,3},{5,4},{6,5},{7,6},{8,7},{9,8},{10,9},{11,1... | collective-permute-start | bytes 49160 | tf_op jit(solution)/shard_map/while/body/eval_jaxpr/ppermute | solution.py:28
  129.6 10.0 %collective-permute-start.1 = (f32[2,2,1024]{2,1,0:T(2,128)S(1)}, f32[2,2,1024]{2,1,0:T(2,128)S(1)}, u32[]{:S(2)}, u32[]{:S(2)}) collective-permute-start(f32[2,2,1024]{2,1,0:T(2,128)S(1)} %get-tuple-element.344), channel_id=1, source_target_pairs={{0,1},{1,2},{2,3},{3,4},{4,5},{5,6},{6,7},{7,8},{8,9},{9,10},{10,1... | collective-permute-start | bytes 49160 | tf_op jit(solution)/shard_map/while/body/eval_jaxpr/ppermute | solution.py:25
  141.1 5.9 %collective-permute-start = (f32[2,2,1024]{2,1,0:T(2,128)S(1)}, f32[2,2,1024]{2,1,0:T(2,128)S(1)}, u32[]{:S(2)}, u32[]{:S(2)}) collective-permute-start(f32[2,2,1024]{2,1,0:T(2,128)S(1)} %get-tuple-element.343), channel_id=1, source_target_pairs={{1,0},{2,1},{3,2},{4,3},{5,4},{6,5},{7,6},{8,7},{9,8},{10,9},{11,1... | collective-permute-start | bytes 49160 | tf_op jit(solution)/shard_map/while/body/eval_jaxpr/ppermute | solution.py:28
  143.0 10.0 %collective-permute-start.1 = (f32[2,2,1024]{2,1,0:T(2,128)S(1)}, f32[2,2,1024]{2,1,0:T(2,128)S(1)}, u32[]{:S(2)}, u32[]{:S(2)}) collective-permute-start(f32[2,2,1024]{2,1,0:T(2,128)S(1)} %get-tuple-element.344), channel_id=1, source_target_pairs={{0,1},{1,2},{2,3},{3,4},{4,5},{5,6},{6,7},{7,8},{8,9},{9,10},{10,1... | collective-permute-start | bytes 49160 | tf_op jit(solution)/shard_map/while/body/eval_jaxpr/ppermute | solution.py:25
  154.5 5.9 %collective-permute-start = (f32[2,2,1024]{2,1,0:T(2,128)S(1)}, f32[2,2,1024]{2,1,0:T(2,128)S(1)}, u32[]{:S(2)}, u32[]{:S(2)}) collective-permute-start(f32[2,2,1024]{2,1,0:T(2,128)S(1)} %get-tuple-element.343), channel_id=1, source_target_pairs={{1,0},{2,1},{3,2},{4,3},{5,4},{6,5},{7,6},{8,7},{9,8},{10,9},{11,1... | collective-permute-start | bytes 49160 | tf_op jit(solution)/shard_map/while/body/eval_jaxpr/ppermute | solution.py:28
  156.4 10.0 %collective-permute-start.1 = (f32[2,2,1024]{2,1,0:T(2,128)S(1)}, f32[2,2,1024]{2,1,0:T(2,128)S(1)}, u32[]{:S(2)}, u32[]{:S(2)}) collective-permute-start(f32[2,2,1024]{2,1,0:T(2,128)S(1)} %get-tuple-element.344), channel_id=1, source_target_pairs={{0,1},{1,2},{2,3},{3,4},{4,5},{5,6},{6,7},{7,8},{8,9},{9,10},{10,1... | collective-permute-start | bytes 49160 | tf_op jit(solution)/shard_map/while/body/eval_jaxpr/ppermute | solution.py:25
  168.0 5.9 %collective-permute-start = (f32[2,2,1024]{2,1,0:T(2,128)S(1)}, f32[2,2,1024]{2,1,0:T(2,128)S(1)}, u32[]{:S(2)}, u32[]{:S(2)}) collective-permute-start(f32[2,2,1024]{2,1,0:T(2,128)S(1)} %get-tuple-element.343), channel_id=1, source_target_pairs={{1,0},{2,1},{3,2},{4,3},{5,4},{6,5},{7,6},{8,7},{9,8},{10,9},{11,1... | collective-permute-start | bytes 49160 | tf_op jit(solution)/shard_map/while/body/eval_jaxpr/ppermute | solution.py:28
  169.9 10.0 %collective-permute-start.1 = (f32[2,2,1024]{2,1,0:T(2,128)S(1)}, f32[2,2,1024]{2,1,0:T(2,128)S(1)}, u32[]{:S(2)}, u32[]{:S(2)}) collective-permute-start(f32[2,2,1024]{2,1,0:T(2,128)S(1)} %get-tuple-element.344), channel_id=1, source_target_pairs={{0,1},{1,2},{2,3},{3,4},{4,5},{5,6},{6,7},{7,8},{8,9},{9,10},{10,1... | collective-permute-start | bytes 49160 | tf_op jit(solution)/shard_map/while/body/eval_jaxpr/ppermute | solution.py:25
  181.4 5.9 %collective-permute-start = (f32[2,2,1024]{2,1,0:T(2,128)S(1)}, f32[2,2,1024]{2,1,0:T(2,128)S(1)}, u32[]{:S(2)}, u32[]{:S(2)}) collective-permute-start(f32[2,2,1024]{2,1,0:T(2,128)S(1)} %get-tuple-element.343), channel_id=1, source_target_pairs={{1,0},{2,1},{3,2},{4,3},{5,4},{6,5},{7,6},{8,7},{9,8},{10,9},{11,1... | collective-permute-start | bytes 49160 | tf_op jit(solution)/shard_map/while/body/eval_jaxpr/ppermute | solution.py:28
  183.3 10.0 %collective-permute-start.1 = (f32[2,2,1024]{2,1,0:T(2,128)S(1)}, f32[2,2,1024]{2,1,0:T(2,128)S(1)}, u32[]{:S(2)}, u32[]{:S(2)}) collective-permute-start(f32[2,2,1024]{2,1,0:T(2,128)S(1)} %get-tuple-element.344), channel_id=1, source_target_pairs={{0,1},{1,2},{2,3},{3,4},{4,5},{5,6},{6,7},{7,8},{8,9},{9,10},{10,1... | collective-permute-start | bytes 49160 | tf_op jit(solution)/shard_map/while/body/eval_jaxpr/ppermute | solution.py:25
  194.9 5.9 %collective-permute-start = (f32[2,2,1024]{2,1,0:T(2,128)S(1)}, f32[2,2,1024]{2,1,0:T(2,128)S(1)}, u32[]{:S(2)}, u32[]{:S(2)}) collective-permute-start(f32[2,2,1024]{2,1,0:T(2,128)S(1)} %get-tuple-element.343), channel_id=1, source_target_pairs={{1,0},{2,1},{3,2},{4,3},{5,4},{6,5},{7,6},{8,7},{9,8},{10,9},{11,1... | collective-permute-start | bytes 49160 | tf_op jit(solution)/shard_map/while/body/eval_jaxpr/ppermute | solution.py:28
  196.8 10.0 %collective-permute-start.1 = (f32[2,2,1024]{2,1,0:T(2,128)S(1)}, f32[2,2,1024]{2,1,0:T(2,128)S(1)}, u32[]{:S(2)}, u32[]{:S(2)}) collective-permute-start(f32[2,2,1024]{2,1,0:T(2,128)S(1)} %get-tuple-element.344), channel_id=1, source_target_pairs={{0,1},{1,2},{2,3},{3,4},{4,5},{5,6},{6,7},{7,8},{8,9},{9,10},{10,1... | collective-permute-start | bytes 49160 | tf_op jit(solution)/shard_map/while/body/eval_jaxpr/ppermute | solution.py:25
  208.3 5.9 %collective-permute-start = (f32[2,2,1024]{2,1,0:T(2,128)S(1)}, f32[2,2,1024]{2,1,0:T(2,128)S(1)}, u32[]{:S(2)}, u32[]{:S(2)}) collective-permute-start(f32[2,2,1024]{2,1,0:T(2,128)S(1)} %get-tuple-element.343), channel_id=1, source_target_pairs={{1,0},{2,1},{3,2},{4,3},{5,4},{6,5},{7,6},{8,7},{9,8},{10,9},{11,1... | collective-permute-start | bytes 49160 | tf_op jit(solution)/shard_map/while/body/eval_jaxpr/ppermute | solution.py:28
  210.3 10.0 %collective-permute-start.1 = (f32[2,2,1024]{2,1,0:T(2,128)S(1)}, f32[2,2,1024]{2,1,0:T(2,128)S(1)}, u32[]{:S(2)}, u32[]{:S(2)}) collective-permute-start(f32[2,2,1024]{2,1,0:T(2,128)S(1)} %get-tuple-element.344), channel_id=1, source_target_pairs={{0,1},{1,2},{2,3},{3,4},{4,5},{5,6},{6,7},{7,8},{8,9},{9,10},{10,1... | collective-permute-start | bytes 49160 | tf_op jit(solution)/shard_map/while/body/eval_jaxpr/ppermute | solution.py:25
  221.8 5.9 %collective-permute-start = (f32[2,2,1024]{2,1,0:T(2,128)S(1)}, f32[2,2,1024]{2,1,0:T(2,128)S(1)}, u32[]{:S(2)}, u32[]{:S(2)}) collective-permute-start(f32[2,2,1024]{2,1,0:T(2,128)S(1)} %get-tuple-element.343), channel_id=1, source_target_pairs={{1,0},{2,1},{3,2},{4,3},{5,4},{6,5},{7,6},{8,7},{9,8},{10,9},{11,1... | collective-permute-start | bytes 49160 | tf_op jit(solution)/shard_map/while/body/eval_jaxpr/ppermute | solution.py:28
  223.7 10.0 %collective-permute-start.1 = (f32[2,2,1024]{2,1,0:T(2,128)S(1)}, f32[2,2,1024]{2,1,0:T(2,128)S(1)}, u32[]{:S(2)}, u32[]{:S(2)}) collective-permute-start(f32[2,2,1024]{2,1,0:T(2,128)S(1)} %get-tuple-element.344), channel_id=1, source_target_pairs={{0,1},{1,2},{2,3},{3,4},{4,5},{5,6},{6,7},{7,8},{8,9},{9,10},{10,1... | collective-permute-start | bytes 49160 | tf_op jit(solution)/shard_map/while/body/eval_jaxpr/ppermute | solution.py:25
  235.2 5.9 %collective-permute-start = (f32[2,2,1024]{2,1,0:T(2,128)S(1)}, f32[2,2,1024]{2,1,0:T(2,128)S(1)}, u32[]{:S(2)}, u32[]{:S(2)}) collective-permute-start(f32[2,2,1024]{2,1,0:T(2,128)S(1)} %get-tuple-element.343), channel_id=1, source_target_pairs={{1,0},{2,1},{3,2},{4,3},{5,4},{6,5},{7,6},{8,7},{9,8},{10,9},{11,1... | collective-permute-start | bytes 49160 | tf_op jit(solution)/shard_map/while/body/eval_jaxpr/ppermute | solution.py:28
  237.1 10.0 %collective-permute-start.1 = (f32[2,2,1024]{2,1,0:T(2,128)S(1)}, f32[2,2,1024]{2,1,0:T(2,128)S(1)}, u32[]{:S(2)}, u32[]{:S(2)}) collective-permute-start(f32[2,2,1024]{2,1,0:T(2,128)S(1)} %get-tuple-element.344), channel_id=1, source_target_pairs={{0,1},{1,2},{2,3},{3,4},{4,5},{5,6},{6,7},{7,8},{8,9},{9,10},{10,1... | collective-permute-start | bytes 49160 | tf_op jit(solution)/shard_map/while/body/eval_jaxpr/ppermute | solution.py:25
  248.7 5.9 %collective-permute-start = (f32[2,2,1024]{2,1,0:T(2,128)S(1)}, f32[2,2,1024]{2,1,0:T(2,128)S(1)}, u32[]{:S(2)}, u32[]{:S(2)}) collective-permute-start(f32[2,2,1024]{2,1,0:T(2,128)S(1)} %get-tuple-element.343), channel_id=1, source_target_pairs={{1,0},{2,1},{3,2},{4,3},{5,4},{6,5},{7,6},{8,7},{9,8},{10,9},{11,1... | collective-permute-start | bytes 49160 | tf_op jit(solution)/shard_map/while/body/eval_jaxpr/ppermute | solution.py:28
  250.6 10.0 %collective-permute-start.1 = (f32[2,2,1024]{2,1,0:T(2,128)S(1)}, f32[2,2,1024]{2,1,0:T(2,128)S(1)}, u32[]{:S(2)}, u32[]{:S(2)}) collective-permute-start(f32[2,2,1024]{2,1,0:T(2,128)S(1)} %get-tuple-element.344), channel_id=1, source_target_pairs={{0,1},{1,2},{2,3},{3,4},{4,5},{5,6},{6,7},{7,8},{8,9},{9,10},{10,1... | collective-permute-start | bytes 49160 | tf_op jit(solution)/shard_map/while/body/eval_jaxpr/ppermute | solution.py:25
  262.1 5.9 %collective-permute-start = (f32[2,2,1024]{2,1,0:T(2,128)S(1)}, f32[2,2,1024]{2,1,0:T(2,128)S(1)}, u32[]{:S(2)}, u32[]{:S(2)}) collective-permute-start(f32[2,2,1024]{2,1,0:T(2,128)S(1)} %get-tuple-element.343), channel_id=1, source_target_pairs={{1,0},{2,1},{3,2},{4,3},{5,4},{6,5},{7,6},{8,7},{9,8},{10,9},{11,1... | collective-permute-start | bytes 49160 | tf_op jit(solution)/shard_map/while/body/eval_jaxpr/ppermute | solution.py:28
  264.0 10.0 %collective-permute-start.1 = (f32[2,2,1024]{2,1,0:T(2,128)S(1)}, f32[2,2,1024]{2,1,0:T(2,128)S(1)}, u32[]{:S(2)}, u32[]{:S(2)}) collective-permute-start(f32[2,2,1024]{2,1,0:T(2,128)S(1)} %get-tuple-element.344), channel_id=1, source_target_pairs={{0,1},{1,2},{2,3},{3,4},{4,5},{5,6},{6,7},{7,8},{8,9},{9,10},{10,1... | collective-permute-start | bytes 49160 | tf_op jit(solution)/shard_map/while/body/eval_jaxpr/ppermute | solution.py:25
  275.5 5.9 %collective-permute-start = (f32[2,2,1024]{2,1,0:T(2,128)S(1)}, f32[2,2,1024]{2,1,0:T(2,128)S(1)}, u32[]{:S(2)}, u32[]{:S(2)}) collective-permute-start(f32[2,2,1024]{2,1,0:T(2,128)S(1)} %get-tuple-element.343), channel_id=1, source_target_pairs={{1,0},{2,1},{3,2},{4,3},{5,4},{6,5},{7,6},{8,7},{9,8},{10,9},{11,1... | collective-permute-start | bytes 49160 | tf_op jit(solution)/shard_map/while/body/eval_jaxpr/ppermute | solution.py:28
  277.5 10.0 %collective-permute-start.1 = (f32[2,2,1024]{2,1,0:T(2,128)S(1)}, f32[2,2,1024]{2,1,0:T(2,128)S(1)}, u32[]{:S(2)}, u32[]{:S(2)}) collective-permute-start(f32[2,2,1024]{2,1,0:T(2,128)S(1)} %get-tuple-element.344), channel_id=1, source_target_pairs={{0,1},{1,2},{2,3},{3,4},{4,5},{5,6},{6,7},{7,8},{8,9},{9,10},{10,1... | collective-permute-start | bytes 49160 | tf_op jit(solution)/shard_map/while/body/eval_jaxpr/ppermute | solution.py:25
  289.0 5.9 %collective-permute-start = (f32[2,2,1024]{2,1,0:T(2,128)S(1)}, f32[2,2,1024]{2,1,0:T(2,128)S(1)}, u32[]{:S(2)}, u32[]{:S(2)}) collective-permute-start(f32[2,2,1024]{2,1,0:T(2,128)S(1)} %get-tuple-element.343), channel_id=1, source_target_pairs={{1,0},{2,1},{3,2},{4,3},{5,4},{6,5},{7,6},{8,7},{9,8},{10,9},{11,1... | collective-permute-start | bytes 49160 | tf_op jit(solution)/shard_map/while/body/eval_jaxpr/ppermute | solution.py:28
  290.9 10.0 %collective-permute-start.1 = (f32[2,2,1024]{2,1,0:T(2,128)S(1)}, f32[2,2,1024]{2,1,0:T(2,128)S(1)}, u32[]{:S(2)}, u32[]{:S(2)}) collective-permute-start(f32[2,2,1024]{2,1,0:T(2,128)S(1)} %get-tuple-element.344), channel_id=1, source_target_pairs={{0,1},{1,2},{2,3},{3,4},{4,5},{5,6},{6,7},{7,8},{8,9},{9,10},{10,1... | collective-permute-start | bytes 49160 | tf_op jit(solution)/shard_map/while/body/eval_jaxpr/ppermute | solution.py:25
  302.4 5.9 %collective-permute-start = (f32[2,2,1024]{2,1,0:T(2,128)S(1)}, f32[2,2,1024]{2,1,0:T(2,128)S(1)}, u32[]{:S(2)}, u32[]{:S(2)}) collective-permute-start(f32[2,2,1024]{2,1,0:T(2,128)S(1)} %get-tuple-element.343), channel_id=1, source_target_pairs={{1,0},{2,1},{3,2},{4,3},{5,4},{6,5},{7,6},{8,7},{9,8},{10,9},{11,1... | collective-permute-start | bytes 49160 | tf_op jit(solution)/shard_map/while/body/eval_jaxpr/ppermute | solution.py:28
  304.3 10.0 %collective-permute-start.1 = (f32[2,2,1024]{2,1,0:T(2,128)S(1)}, f32[2,2,1024]{2,1,0:T(2,128)S(1)}, u32[]{:S(2)}, u32[]{:S(2)}) collective-permute-start(f32[2,2,1024]{2,1,0:T(2,128)S(1)} %get-tuple-element.344), channel_id=1, source_target_pairs={{0,1},{1,2},{2,3},{3,4},{4,5},{5,6},{6,7},{7,8},{8,9},{9,10},{10,1... | collective-permute-start | bytes 49160 | tf_op jit(solution)/shard_map/while/body/eval_jaxpr/ppermute | solution.py:25
  315.8 5.9 %collective-permute-start = (f32[2,2,1024]{2,1,0:T(2,128)S(1)}, f32[2,2,1024]{2,1,0:T(2,128)S(1)}, u32[]{:S(2)}, u32[]{:S(2)}) collective-permute-start(f32[2,2,1024]{2,1,0:T(2,128)S(1)} %get-tuple-element.343), channel_id=1, source_target_pairs={{1,0},{2,1},{3,2},{4,3},{5,4},{6,5},{7,6},{8,7},{9,8},{10,9},{11,1... | collective-permute-start | bytes 49160 | tf_op jit(solution)/shard_map/while/body/eval_jaxpr/ppermute | solution.py:28
  317.7 10.0 %collective-permute-start.1 = (f32[2,2,1024]{2,1,0:T(2,128)S(1)}, f32[2,2,1024]{2,1,0:T(2,128)S(1)}, u32[]{:S(2)}, u32[]{:S(2)}) collective-permute-start(f32[2,2,1024]{2,1,0:T(2,128)S(1)} %get-tuple-element.344), channel_id=1, source_target_pairs={{0,1},{1,2},{2,3},{3,4},{4,5},{5,6},{6,7},{7,8},{8,9},{9,10},{10,1... | collective-permute-start | bytes 49160 | tf_op jit(solution)/shard_map/while/body/eval_jaxpr/ppermute | solution.py:25
  329.2 5.9 %collective-permute-start = (f32[2,2,1024]{2,1,0:T(2,128)S(1)}, f32[2,2,1024]{2,1,0:T(2,128)S(1)}, u32[]{:S(2)}, u32[]{:S(2)}) collective-permute-start(f32[2,2,1024]{2,1,0:T(2,128)S(1)} %get-tuple-element.343), channel_id=1, source_target_pairs={{1,0},{2,1},{3,2},{4,3},{5,4},{6,5},{7,6},{8,7},{9,8},{10,9},{11,1... | collective-permute-start | bytes 49160 | tf_op jit(solution)/shard_map/while/body/eval_jaxpr/ppermute | solution.py:28
  331.1 10.0 %collective-permute-start.1 = (f32[2,2,1024]{2,1,0:T(2,128)S(1)}, f32[2,2,1024]{2,1,0:T(2,128)S(1)}, u32[]{:S(2)}, u32[]{:S(2)}) collective-permute-start(f32[2,2,1024]{2,1,0:T(2,128)S(1)} %get-tuple-element.344), channel_id=1, source_target_pairs={{0,1},{1,2},{2,3},{3,4},{4,5},{5,6},{6,7},{7,8},{8,9},{9,10},{10,1... | collective-permute-start | bytes 49160 | tf_op jit(solution)/shard_map/while/body/eval_jaxpr/ppermute | solution.py:25
where the time goes:
time: 347 us; the launch traced here: 345 us
  starting transfers between devices  130 us (37%)
  waiting for transfers between devices  100 us (29%)
  local copies, waits for them, and re-layouts  63.5 us (18%)
  other arithmetic  25.4 us (7%)
  blocking collectives  22.7 us (7%)
    ppermute x18, waiting for transfers between devices, with_halo(): lax.ppermute(lax.slice_in_dim(block, block.shape[dim] - width, None, axis...  100 us
    ppermute x18, starting transfers between devices, with_halo(): lax.ppermute(lax.slice_in_dim(block, block.shape[dim] - width, None, axis...  66.2 us
    ppermute x18, starting transfers between devices, with_halo(): lax.ppermute(lax.slice_in_dim(block, 0, width, axis=dim), axis, backward)  57.7 us
    another operation x5, local copies, waits for them, and re-layouts, reaction(): return jnp.stack([new_first, new_second], axis=0)  30.8 us
    all_gather x1, blocking collectives, broadcast(): lax.all_gather(array, axis)  22.7 us
    reshape x1, local copies, waits for them, and re-layouts, restrict_flat(): fields.reshape(2, extent[1] // COARSEN, COARSEN, extent[2] // COARSEN, CO...  18.1 us
    another operation x149, other arithmetic, reaction(): return jnp.stack([new_first, new_second], axis=0)  9.7 us
    reduce_sum x2, other arithmetic, restrict_flat(): means = jnp.mean(blocks, axis=(2, 4, 6))  7.06 us
  transfers between devices with their start and end apart: 37, of which 17 were waited for; matrix products, arithmetic and copies ran while one was open for 1% of the time, Pallas kernels for 0%

commit v1 on v0

v1 whole, which is shorter than its diff:
```python
import jax
import jax.numpy as jnp
from jax import lax
from jax.experimental import pallas as pl
from jax.experimental.pallas import tpu as pltpu
from jax.sharding import PartitionSpec as P

MESH = pl.DeviceIdType.MESH
GY = 32
GZ = 128
CY = GY // 2
PLANES = 8
COARSE = PLANES // 2
HALO = 4
PADDED = PLANES + 2 * HALO

SPREAD_FIRST = 0.14
SPREAD_SECOND = 0.13
FEED_RATE = 0.035
KILL_RATE = 0.065


def even_lanes(shape):
    return lax.broadcasted_iota(jnp.int32, shape, len(shape) - 1) % 2 == 0


def coarse_step(x):
    inner = x[1:-1]
    even = even_lanes(inner.shape)
    beside = x[2:] + x[:-2]
    beside = beside + pltpu.roll(inner, 1, 1) + pltpu.roll(inner, CY - 1, 1)
    beside = beside + pltpu.roll(inner, 2, 2) + pltpu.roll(inner, GZ - 2, 2)
    other = jnp.where(even, pltpu.roll(inner, GZ - 1, 2), pltpu.roll(inner, 1, 2))
    second = jnp.where(even, other, inner)
    feeding = inner * other * second
    spread = jnp.where(even, 0.5 * SPREAD_FIRST, 0.5 * SPREAD_SECOND)
    keep = jnp.where(
        even,
        1.0 - 3.0 * SPREAD_FIRST - 2.0 * FEED_RATE,
        1.0 - 3.0 * SPREAD_SECOND - 2.0 * (FEED_RATE + KILL_RATE),
    )
    gain = jnp.where(even, 2.0 * FEED_RATE, 0.0)
    sign = jnp.where(even, -2.0, 2.0)
    return keep * inner + spread * beside + gain + sign * feeding


def march(x):
    return coarse_step(coarse_step(x))


def fine_planes(source, target, first, count):
    def body(step, carry):
        p = first + step
        u = source[0, p]
        v = source[1, p]
        feeding = u * v * v
        beside = source[0, p - 1] + source[0, p + 1]
        beside = beside + pltpu.roll(u, 1, 0) + pltpu.roll(u, GY - 1, 0)
        beside = beside + pltpu.roll(u, 1, 1) + pltpu.roll(u, GZ - 1, 1)
        target[0, p] = (
            (1.0 - 6.0 * SPREAD_FIRST - FEED_RATE) * u + SPREAD_FIRST * beside + FEED_RATE - feeding
        )
        beside = source[1, p - 1] + source[1, p + 1]
        beside = beside + pltpu.roll(v, 1, 0) + pltpu.roll(v, GY - 1, 0)
        beside = beside + pltpu.roll(v, 1, 1) + pltpu.roll(v, GZ - 1, 1)
        target[1, p] = (
            (1.0 - 6.0 * SPREAD_SECOND - FEED_RATE - KILL_RATE) * v
            + SPREAD_SECOND * beside
            + feeding
        )
        return carry

    lax.fori_loop(0, count, body, 0, unroll=2)


def restrict(source, first, rows, out, count):
    def body(i, carry):
        p = first + 2 * i
        u = source[0, p] + source[0, p + 1]
        v = source[1, p] + source[1, p + 1]
        even = even_lanes(u.shape)
        rows[i] = jnp.where(even, u + pltpu.roll(u, GZ - 1, 1), v + pltpu.roll(v, 1, 1))
        out[i] = 0.125 * (rows[i, pl.ds(0, CY, stride=2)] + rows[i, pl.ds(1, CY, stride=2)])
        return carry

    lax.fori_loop(0, count, body, 0)


def kernel(
    cuts,
    space,
    u_ref,
    v_ref,
    out_u,
    out_v,
    fine,
    rows,
    start_coarse,
    end_coarse,
    mine,
    terms,
    states,
    halos,
    wings,
    fine_send,
    fine_recv,
    term_send,
    term_recv,
    halo_send,
    halo_recv,
    wing_send,
    wing_recv,
):
    n = lax.axis_index("cuts")
    s = lax.axis_index("space")
    right = {"space": lax.rem(s + 1, space)}
    left = {"space": lax.rem(s + space - 1, space)}
    rounds = cuts // 2

    barrier = pltpu.get_barrier_semaphore()
    for side in (left, right):
        pl.semaphore_signal(barrier, inc=1, device_id=side, device_id_type=MESH)
    for d in range(1, cuts):
        pl.semaphore_signal(
            barrier, inc=1, device_id={"cuts": lax.rem(n + d, cuts)}, device_id_type=MESH
        )
    pl.semaphore_wait(barrier, cuts + 1)

    def remote(source, target, send, recv, device):
        return pltpu.make_async_remote_copy(
            src_ref=source,
            dst_ref=target,
            send_sem=send,
            recv_sem=recv,
            device_id=device,
            device_id_type=MESH,
        )

    now = fine.at[0]
    copies = []
    for k, ref in enumerate((u_ref, v_ref)):
        copies.append(
            remote(
                ref.at[0, pl.ds(PLANES - HALO, HALO)],
                now.at[k, pl.ds(0, HALO)],
                fine_send.at[2 * k],
                fine_recv.at[2 * k],
                right,
            )
        )
        copies.append(
            remote(
                ref.at[0, pl.ds(0, HALO)],
                now.at[k, pl.ds(HALO + PLANES, HALO)],
                fine_send.at[2 * k + 1],
                fine_recv.at[2 * k + 1],
                left,
            )
        )
    for copy in copies:
        copy.start()
    fine[0, 0, pl.ds(HALO, PLANES)] = u_ref[0]
    fine[0, 1, pl.ds(HALO, PLANES)] = v_ref[0]
    for copy in copies:
        copy.wait()

    restrict(now, 0, rows, start_coarse, PADDED // 2)
    for t in range(4):
        fine_planes(fine.at[t % 2], fine.at[(t + 1) % 2], t + 1, PADDED - 2 - 2 * t)
    restrict(now, HALO, rows, end_coarse, COARSE)
    finish = end_coarse[...]
    correction = finish - march(start_coarse[...])
    terms[n] = jnp.where(n == 0, finish, correction)

    def term_copy(d):
        return remote(
            terms.at[n],
            terms.at[n],
            term_send.at[d],
            term_recv.at[n],
            {"cuts": lax.rem(n + d, cuts)},
        )

    for d in range(1, cuts):
        term_copy(d).start()

    def await_term(m):
        @pl.when(n != m)
        def _():
            remote(
                terms.at[m], terms.at[m], term_send.at[0], term_recv.at[m], right
            ).wait_recv()

    def halo_copies(source, r):
        return (
            remote(source, halos.at[r, 0], halo_send.at[r, 0], halo_recv.at[r, 0], right),
            remote(source, halos.at[r, 1], halo_send.at[r, 1], halo_recv.at[r, 1], left),
        )

    def wing_copies(r):
        return (
            remote(
                terms.at[2 * r, pl.ds(2, 2)],
                wings.at[r, 0],
                wing_send.at[r, 0],
                wing_recv.at[r, 0],
                right,
            ),
            remote(
                terms.at[2 * r, pl.ds(0, 2)],
                wings.at[r, 1],
                wing_send.at[r, 1],
                wing_recv.at[r, 1],
                left,
            ),
        )

    def keep(m, state):
        @pl.when(n == m)
        def _():
            mine[...] = state

    await_term(0)
    exchange = halo_copies(terms.at[0], 0)
    for copy in exchange:
        copy.start()
    keep(0, terms[0])
    await_term(2)
    for copy in wing_copies(1):
        copy.start()
    await_term(1)
    for copy in exchange:
        copy.wait()
    state = jnp.concatenate([halos[0, 0, 2:], terms[0], halos[0, 1, :2]], axis=0)
    state = march(state) + terms[1]
    states[1] = state
    keep(1, state)

    def one_round(r, carry):
        sent = halo_copies(states.at[r], r)
        for copy in sent:
            copy.start()

        @pl.when(r < rounds - 1)
        def _():
            await_term(2 * r + 2)
            for copy in wing_copies(r + 1):
                copy.start()

        await_term(2 * r + 1)
        for copy in wing_copies(r):
            copy.wait()
        for copy in sent:
            copy.wait()
        wide = jnp.concatenate([halos[r, 0], states[r], halos[r, 1]], axis=0)
        term = jnp.concatenate([wings[r, 0], terms[2 * r], wings[r, 1]], axis=0)
        wide = march(wide) + term
        keep(2 * r, wide[2:6])
        state = march(wide) + terms[2 * r + 1]
        states[r + 1] = state
        keep(2 * r + 1, state)
        return carry

    lax.fori_loop(1, rounds, one_round, 0)

    change = mine[...] - end_coarse[...]
    even = even_lanes(change.shape)
    for k, (out, spread) in enumerate(
        (
            (out_u, jnp.where(even, change, pltpu.roll(change, 1, 2))),
            (out_v, jnp.where(even, pltpu.roll(change, GZ - 1, 2), change)),
        )
    ):
        for i in range(COARSE):
            slot = k * COARSE + i
            rows[slot, pl.ds(0, CY, stride=2)] = spread[i]
            rows[slot, pl.ds(1, CY, stride=2)] = spread[i]
            added = rows[slot]
            out[0, 2 * i] = fine[0, k, HALO + 2 * i] + added
            out[0, 2 * i + 1] = fine[0, k, HALO + 2 * i + 1] + added

    for d in range(1, cuts):
        term_copy(d).wait_send()


def on_device(start_u, start_v):
    cuts = lax.axis_size("cuts")
    space = lax.axis_size("space")
    rounds = cuts // 2
    block = (COARSE, CY, GZ)
    f32 = jnp.float32
    shape = jax.ShapeDtypeStruct((1, PLANES, GY, GZ), f32)
    vmem = pl.BlockSpec(memory_space=pltpu.VMEM)
    dma = pltpu.SemaphoreType.DMA

    def body(*refs):
        kernel(cuts, space, *refs)

    return pl.pallas_call(
        body,
        out_shape=(shape, shape),
        in_specs=[vmem, vmem],
        out_specs=(vmem, vmem),
        scratch_shapes=[
            pltpu.VMEM((2, 2, PADDED, GY, GZ), f32),
            pltpu.VMEM((PADDED // 2, GY, GZ), f32),
            pltpu.VMEM((PADDED // 2, CY, GZ), f32),
            pltpu.VMEM(block, f32),
            pltpu.VMEM(block, f32),
            pltpu.VMEM((cuts, *block), f32),
            pltpu.VMEM((rounds + 1, *block), f32),
            pltpu.VMEM((rounds, 2, *block), f32),
            pltpu.VMEM((rounds, 2, 2, CY, GZ), f32),
            dma((4,)),
            dma((4,)),
            dma((cuts,)),
            dma((cuts,)),
            dma((rounds, 2)),
            dma((rounds, 2)),
            dma((rounds, 2)),
            dma((rounds, 2)),
        ],
        compiler_params=pltpu.CompilerParams(collective_id=0, has_side_effects=True),
        name="parareal",
    )(start_u, start_v)


def solution(mesh):
    return jax.shard_map(
        on_device,
        mesh=mesh,
        in_specs=(P("cuts", "space", None, None), P("cuts", "space", None, None)),
        out_specs=(P("cuts", "space", None, None), P("cuts", "space", None, None)),
        check_vma=False,
    )
```

time: 347 us -> 85.7 us (0.25)
  the two profiles are of different devices: /device:TPU:64 before, /device:TPU:70 now
where the time goes in v1:
time: 85.7 us; the launch traced here: 85.5 us
  Pallas kernels  82.6 us (96%)
  local copies, waits for them, and re-layouts  2.26 us (3%)
    pallas_call x1, Pallas kernels, on_device(): pl.pallas_call(body, out_shape=(shape, shape), in_specs=[vmem, vmem], out...  82.6 us
    unnamed x4, local copies, waits for them, and re-layouts  2.26 us

profile of v1, /device:TPU:70, one launch (start us, length us, event | category | flops | bytes accessed | tf_op | source)
XLA Modules:
  0.0 85.5 jit_solution(5122779495204687739)
XLA Ops:
  0.6 82.6 %parareal.1 = (f32[1,8,32,128]{3,2,1,0:T(8,128)}, f32[1,8,32,128]{3,2,1,0:T(8,128)}) custom-call(f32[1,8,32,128]{3,2,1,0:T(8,128)} %refs_0_.1, f32[1,8,32,128]{3,2,1,0:T(8,128)} %refs_1_.1), custom_call_target="tpu_custom_call" | custom-call | tf_op jit(solution)/shard_map/parareal/pallas_call | solution.py:299
  83.2 0.0 copy-start
  83.2 1.6 %copy.6 = f32[1,8,32,128]{3,2,1,0:T(8,128)} copy(f32[1,8,32,128]{3,2,1,0:T(8,128)} %get-tuple-element.4) | data formatting | bytes 262144
  84.8 0.0 copy-done
  84.9 0.7 copy.7
Async XLA Ops:
  83.2 1.6 %copy-start = (f32[1,8,32,128]{3,2,1,0:T(8,128)S(1)}, f32[1,8,32,128]{3,2,1,0:T(8,128)}, u32[]{:S(2)}) copy-start(f32[1,8,32,128]{3,2,1,0:T(8,128)} %get-tuple-element.5) | copy-start | bytes 393220

commit v2 on v1

v2 whole, which is shorter than its diff:
```python
import jax
import jax.numpy as jnp
from jax import lax
from jax.experimental import pallas as pl
from jax.experimental.pallas import tpu as pltpu
from jax.sharding import PartitionSpec as P

MESH = pl.DeviceIdType.MESH
GY = 32
GZ = 128
CY = GY // 2
PLANES = 8
COARSE = PLANES // 2
HALO = 4
PADDED = PLANES + 2 * HALO

SPREAD_FIRST = 0.14
SPREAD_SECOND = 0.13
FEED_RATE = 0.035
KILL_RATE = 0.065


def even_lanes(shape):
    return lax.broadcasted_iota(jnp.int32, shape, len(shape) - 1) % 2 == 0


def coarse_step(x):
    inner = x[1:-1]
    even = even_lanes(inner.shape)
    beside = x[2:] + x[:-2]
    beside = beside + pltpu.roll(inner, 1, 1) + pltpu.roll(inner, CY - 1, 1)
    beside = beside + pltpu.roll(inner, 2, 2) + pltpu.roll(inner, GZ - 2, 2)
    other = jnp.where(even, pltpu.roll(inner, GZ - 1, 2), pltpu.roll(inner, 1, 2))
    second = jnp.where(even, other, inner)
    feeding = inner * other * second
    spread = jnp.where(even, 0.5 * SPREAD_FIRST, 0.5 * SPREAD_SECOND)
    keep = jnp.where(
        even,
        1.0 - 3.0 * SPREAD_FIRST - 2.0 * FEED_RATE,
        1.0 - 3.0 * SPREAD_SECOND - 2.0 * (FEED_RATE + KILL_RATE),
    )
    gain = jnp.where(even, 2.0 * FEED_RATE, 0.0)
    sign = jnp.where(even, -2.0, 2.0)
    return keep * inner + spread * beside + gain + sign * feeding


def march(x):
    return coarse_step(coarse_step(x))


def fine_planes(source, target, first, count):
    def body(step, carry):
        p = first + step
        u = source[0, p]
        v = source[1, p]
        feeding = u * v * v
        beside = source[0, p - 1] + source[0, p + 1]
        beside = beside + pltpu.roll(u, 1, 0) + pltpu.roll(u, GY - 1, 0)
        beside = beside + pltpu.roll(u, 1, 1) + pltpu.roll(u, GZ - 1, 1)
        target[0, p] = (
            (1.0 - 6.0 * SPREAD_FIRST - FEED_RATE) * u + SPREAD_FIRST * beside + FEED_RATE - feeding
        )
        beside = source[1, p - 1] + source[1, p + 1]
        beside = beside + pltpu.roll(v, 1, 0) + pltpu.roll(v, GY - 1, 0)
        beside = beside + pltpu.roll(v, 1, 1) + pltpu.roll(v, GZ - 1, 1)
        target[1, p] = (
            (1.0 - 6.0 * SPREAD_SECOND - FEED_RATE - KILL_RATE) * v
            + SPREAD_SECOND * beside
            + feeding
        )
        return carry

    lax.fori_loop(0, count, body, 0, unroll=2)


def restrict(source, first, rows, out, place, count):
    def body(i, carry):
        p = first + 2 * i
        u = source[0, p] + source[0, p + 1]
        v = source[1, p] + source[1, p + 1]
        even = even_lanes(u.shape)
        rows[i] = jnp.where(even, u + pltpu.roll(u, GZ - 1, 1), v + pltpu.roll(v, 1, 1))
        out[place + i] = 0.125 * (
            rows[i, pl.ds(0, CY, stride=2)] + rows[i, pl.ds(1, CY, stride=2)]
        )
        return carry

    lax.fori_loop(0, count, body, 0)


def kernel(
    cuts,
    space,
    u_ref,
    v_ref,
    out_u,
    out_v,
    fine,
    rows,
    start_coarse,
    end_coarse,
    mine,
    slots,
    wides,
    results,
    load_sem,
    fine_send,
    fine_recv,
    term_send,
    term_recv,
    first_send,
    wing_send,
    wing_recv,
    wide_send,
    wide_recv,
    result_send,
    result_recv,
):
    n = lax.axis_index("cuts")
    s = lax.axis_index("space")
    x = lax.rem(n // 2, 4)
    rounds = cuts // 4

    def at(step):
        return lax.rem(s + step + space, space)

    def seat(column, place):
        return lax.rem(place, 8) // 4 * 8 + 2 * column

    chain = n == seat(x, s)
    barrier = pltpu.get_barrier_semaphore()

    def greet(device):
        pl.semaphore_signal(barrier, inc=1, device_id=device, device_id_type=MESH)

    def remote(source, target, send, recv, device):
        return pltpu.make_async_remote_copy(
            src_ref=source,
            dst_ref=target,
            send_sem=send,
            recv_sem=recv,
            device_id=device,
            device_id_type=MESH,
        )

    greet({"space": at(-1)})
    greet({"space": at(1)})
    @pl.when(chain)
    def _():
        for d in range(1, cuts):
            greet({"cuts": lax.rem(n + d, cuts)})
        for step in (-2, -1, 1, 2):
            greet({"cuts": seat(x, at(step)), "space": at(step)})
            greet({"cuts": 0, "space": at(step)})
        for m in (1, 2):
            for step in (-1, 1):
                greet({"cuts": m, "space": at(step)})

    @pl.when(jnp.logical_not(chain))
    def _():
        greet({"cuts": seat(x, s)})

    now = fine.at[0]
    loads = []
    for k, ref in enumerate((u_ref, v_ref)):
        loads.append(
            pltpu.make_async_copy(ref.at[0], now.at[k, pl.ds(HALO, PLANES)], load_sem.at[k])
        )
    for load in loads:
        load.start()

    targets = 2 + 4 + jnp.where(chain, 4 + 3 - 1, 0)
    targets = targets + jnp.where(n == 0, 16, 0) + jnp.where((n == 1) | (n == 2), 8, 0)
    pl.semaphore_wait(barrier, targets)

    copies = []
    for k, ref in enumerate((u_ref, v_ref)):
        copies.append(
            remote(
                ref.at[0, pl.ds(PLANES - HALO, HALO)],
                now.at[k, pl.ds(0, HALO)],
                fine_send.at[2 * k],
                fine_recv.at[2 * k],
                {"space": at(1)},
            )
        )
        copies.append(
            remote(
                ref.at[0, pl.ds(0, HALO)],
                now.at[k, pl.ds(HALO + PLANES, HALO)],
                fine_send.at[2 * k + 1],
                fine_recv.at[2 * k + 1],
                {"space": at(-1)},
            )
        )
    for copy in copies:
        copy.start()
    for load in loads:
        load.wait()

    restrict(now, HALO, rows, start_coarse, 2, COARSE)
    for t in range(3):
        fine_planes(fine.at[t % 2], fine.at[(t + 1) % 2], HALO + 1 + t, PLANES - 2 - 2 * t)
    for copy in copies:
        copy.wait()
    restrict(now, 0, rows, start_coarse, 0, 2)
    restrict(now, HALO + PLANES, rows, start_coarse, COARSE + 2, 2)
    for t in range(3):
        source, target = fine.at[t % 2], fine.at[(t + 1) % 2]
        fine_planes(source, target, t + 1, HALO)
        fine_planes(source, target, PADDED - 1 - HALO - t, HALO)
    fine_planes(fine.at[1], fine.at[0], HALO, PLANES)
    restrict(now, HALO, rows, end_coarse, 0, COARSE)
    finish = end_coarse[...]
    correction = finish - march(start_coarse[...])
    slots[n, pl.ds(6, 4)] = jnp.where(n == 0, finish, correction)

    def term_copy(column):
        return remote(
            slots.at[n, pl.ds(6, 4)],
            slots.at[n, pl.ds(6, 4)],
            term_send.at[column],
            term_recv.at[n],
            {"cuts": seat(column, s)},
        )

    def wing_copy(m, source, target, width, step, side, send, column):
        return remote(
            slots.at[m, pl.ds(6 + source, width)],
            slots.at[m, pl.ds(target, width)],
            send,
            wing_recv.at[m, side],
            {"cuts": seat(column, at(step)), "space": at(step)},
        )

    wings = (
        ((0, 2, 4, 1, 0), (0, 10, 4, -1, 1), (2, 0, 2, 2, 2), (0, 14, 2, -2, 3)),
        ((0, 2, 4, 1, 0), (0, 10, 4, -1, 1)),
        ((2, 4, 2, 1, 0), (0, 10, 2, -1, 1)),
    )

    def first_wings(m):
        return [
            wing_copy(m, *wing, first_send.at[column, wing[4]], column)
            for column in range(4)
            for wing in wings[m]
        ]

    def later_wings(m, kind):
        return [wing_copy(m, *wing, wing_send.at[m, wing[4]], x) for wing in wings[kind]]

    for m in range(3):

        @pl.when(n == m)
        def _():
            for copy in first_wings(m):
                copy.start()

    for column in range(4):

        @pl.when(n != seat(column, s))
        def _():
            term_copy(column).start()

    def await_term(m):
        @pl.when(n != m)
        def _():
            own = slots.at[m, pl.ds(6, 4)]
            remote(own, own, term_send.at[0], term_recv.at[m], {"space": at(1)}).wait_recv()

    def result_copy(m):
        return remote(
            results.at[m], mine, result_send.at[m], result_recv.at[0], {"cuts": m}
        )

    def deliver(m, state):
        @pl.when((lax.rem(m // 2, 4) == x) & (m > 0))
        def _():
            results[m] = state

            @pl.when(m != n)
            def _():
                result_copy(m).start()

    def wide_copies(r):
        return [
            remote(
                wides.at[r, pl.ds(8, 4)],
                wides.at[r, pl.ds(target, 4)],
                wide_send.at[r, side],
                wide_recv.at[r, side],
                {"cuts": seat(x, at(step)), "space": at(step)},
            )
            for target, step, side in ((4, 1, 0), (12, -1, 1), (0, 2, 2), (16, -2, 3))
        ]

    def forward(base):
        for kind in range(3):
            await_term(base + kind)
            for copy in later_wings(base + kind, kind):
                copy.start()

    def three_links(base, wide, r):
        wide = march(wide) + slots[base + 1, 2:14]
        deliver(base + 1, wide[4:8])
        wide = march(wide) + slots[base + 2, 4:12]
        deliver(base + 2, wide[2:6])
        state = march(wide) + slots[base + 3, 6:10]
        wides[r + 1, pl.ds(8, 4)] = state

        @pl.when(r < rounds - 1)
        def _():
            for copy in wide_copies(r + 1):
                copy.start()

        deliver(base + 3, state)

    @pl.when(chain)
    def _():
        for m in range(4):
            await_term(m)
        for m in range(3):
            for copy in (wing_copy(m, *wing, first_send.at[0, wing[4]], x) for wing in wings[m]):
                copy.wait_recv()
        forward(4)
        three_links(0, slots[0], 0)

        def one_round(r, carry):
            base = 4 * r
            for copy in wide_copies(r):
                copy.wait()
            await_term(base + 3)
            for kind in range(3):
                for copy in later_wings(base + kind, kind):
                    copy.wait()

            @pl.when(r < rounds - 1)
            def _():
                forward(base + 4)

            wide = march(wides[r]) + slots[base]
            deliver(base, wide[6:10])
            three_links(base, wide, r)
            return carry

        lax.fori_loop(1, rounds, one_round, 0)
        for m in range(1, cuts):

            @pl.when((m // 2 % 4 == x) & (m != n))
            def _():
                result_copy(m).wait_send()

    @pl.when(n == 0)
    def _():
        mine[...] = end_coarse[...]

    @pl.when(chain & (n > 0))
    def _():
        mine[...] = results[n]

    @pl.when(jnp.logical_not(chain) & (n > 0))
    def _():
        result_copy(n).wait_recv()

    change = mine[...] - end_coarse[...]
    even = even_lanes(change.shape)
    for k, (out, spread) in enumerate(
        (
            (out_u, jnp.where(even, change, pltpu.roll(change, 1, 2))),
            (out_v, jnp.where(even, pltpu.roll(change, GZ - 1, 2), change)),
        )
    ):
        for i in range(COARSE):
            slot = k * COARSE + i
            rows[slot, pl.ds(0, CY, stride=2)] = spread[i]
            rows[slot, pl.ds(1, CY, stride=2)] = spread[i]
            added = rows[slot]
            out[0, 2 * i] = fine[0, k, HALO + 2 * i] + added
            out[0, 2 * i + 1] = fine[0, k, HALO + 2 * i + 1] + added

    for m in range(3):

        @pl.when(n == m)
        def _():
            for copy in first_wings(m):
                copy.wait_send()

    for column in range(4):

        @pl.when(n != seat(column, s))
        def _():
            term_copy(column).wait_send()


def on_device(start_u, start_v):
    cuts = lax.axis_size("cuts")
    space = lax.axis_size("space")
    rounds = cuts // 4
    block = (COARSE, CY, GZ)
    f32 = jnp.float32
    shape = jax.ShapeDtypeStruct((1, PLANES, GY, GZ), f32)
    hbm = pl.BlockSpec(memory_space=pl.ANY)
    vmem = pl.BlockSpec(memory_space=pltpu.VMEM)
    dma = pltpu.SemaphoreType.DMA

    def body(*refs):
        kernel(cuts, space, *refs)

    return pl.pallas_call(
        body,
        out_shape=(shape, shape),
        in_specs=[hbm, hbm],
        out_specs=(vmem, vmem),
        scratch_shapes=[
            pltpu.VMEM((2, 2, PADDED, GY, GZ), f32),
            pltpu.VMEM((PADDED // 2, GY, GZ), f32),
            pltpu.VMEM((PADDED // 2, CY, GZ), f32),
            pltpu.VMEM(block, f32),
            pltpu.VMEM(block, f32),
            pltpu.VMEM((cuts, 16, CY, GZ), f32),
            pltpu.VMEM((rounds + 1, 20, CY, GZ), f32),
            pltpu.VMEM((cuts, *block), f32),
            dma((2,)),
            dma((4,)),
            dma((4,)),
            dma((4,)),
            dma((cuts,)),
            dma((4, 4)),
            dma((cuts, 4)),
            dma((cuts, 4)),
            dma((rounds, 4)),
            dma((rounds, 4)),
            dma((cuts,)),
            dma((1,)),
        ],
        compiler_params=pltpu.CompilerParams(collective_id=0, has_side_effects=True),
        name="parareal",
    )(start_u, start_v)


def solution(mesh):
    return jax.shard_map(
        on_device,
        mesh=mesh,
        in_specs=(P("cuts", "space", None, None), P("cuts", "space", None, None)),
        out_specs=(P("cuts", "space", None, None), P("cuts", "space", None, None)),
        check_vma=False,
    )
```

time: 85.7 us -> 62.4 us (0.73)
  the two profiles are of different devices: /device:TPU:70 before, /device:TPU:6 now
where the time goes in v2:
time: 62.4 us; the launch traced here: 62.2 us
  Pallas kernels  59.3 us (95%)
  local copies, waits for them, and re-layouts  2.26 us (4%)
  between operations  0.65 us (1%)
    pallas_call x1, Pallas kernels, on_device(): pl.pallas_call(body, out_shape=(shape, shape), in_specs=[hbm, hbm], out_s...  59.3 us
    unnamed x4, local copies, waits for them, and re-layouts  2.26 us

profile of v2, /device:TPU:6, one launch (start us, length us, event | category | flops | bytes accessed | tf_op | source)
XLA Modules:
  0.0 62.2 jit_solution(7864683897089176600)
XLA Ops:
  0.6 59.3 %parareal.1 = (f32[1,8,32,128]{3,2,1,0:T(8,128)}, f32[1,8,32,128]{3,2,1,0:T(8,128)}) custom-call(f32[1,8,32,128]{3,2,1,0:T(8,128)} %refs_0_.1, f32[1,8,32,128]{3,2,1,0:T(8,128)} %refs_1_.1), custom_call_target="tpu_custom_call" | custom-call | tf_op jit(solution)/shard_map/parareal/pallas_call | solution.py:409
  60.0 0.0 copy-start
  60.0 1.6 %copy.6 = f32[1,8,32,128]{3,2,1,0:T(8,128)} copy(f32[1,8,32,128]{3,2,1,0:T(8,128)} %get-tuple-element.4) | data formatting | bytes 262144
  61.6 0.0 copy-done
  61.6 0.7 %copy.7 = f32[1,8,32,128]{3,2,1,0:T(8,128)} copy(f32[1,8,32,128]{3,2,1,0:T(8,128)S(1)} %copy-done) | data formatting | bytes 262144
Async XLA Ops:
  60.0 1.6 %copy-start = (f32[1,8,32,128]{3,2,1,0:T(8,128)S(1)}, f32[1,8,32,128]{3,2,1,0:T(8,128)}, u32[]{:S(2)}) copy-start(f32[1,8,32,128]{3,2,1,0:T(8,128)} %get-tuple-element.5) | copy-start | bytes 393220

commit v3 on v2

--- a/solution.py
+++ b/solution.py
@@ -118,16 +118,15 @@
 ):
     n = lax.axis_index("cuts")
     s = lax.axis_index("space")
-    x = lax.rem(n // 2, 4)
     rounds = cuts // 4
 
     def at(step):
         return lax.rem(s + step + space, space)
 
-    def seat(column, place):
-        return lax.rem(place, 8) // 4 * 8 + 2 * column
-
-    chain = n == seat(x, s)
+    def seat(place):
+        return lax.rem(place, 8) // 4 * 8
+
+    chain = n == seat(s)
     barrier = pltpu.get_barrier_semaphore()
 
     def greet(device):
@@ -150,7 +149,7 @@
         for d in range(1, cuts):
             greet({"cuts": lax.rem(n + d, cuts)})
         for step in (-2, -1, 1, 2):
-            greet({"cuts": seat(x, at(step)), "space": at(step)})
+            greet({"cuts": seat(at(step)), "space": at(step)})
             greet({"cuts": 0, "space": at(step)})
         for m in (1, 2):
             for step in (-1, 1):
@@ -158,7 +157,7 @@
 
     @pl.when(jnp.logical_not(chain))
     def _():
-        greet({"cuts": seat(x, s)})
+        greet({"cuts": seat(s)})
 
     now = fine.at[0]
     loads = []
@@ -169,8 +168,8 @@
     for load in loads:
         load.start()
 
-    targets = 2 + 4 + jnp.where(chain, 4 + 3 - 1, 0)
-    targets = targets + jnp.where(n == 0, 16, 0) + jnp.where((n == 1) | (n == 2), 8, 0)
+    targets = 2 + jnp.where(chain, 4 + cuts - 1, 1)
+    targets = targets + jnp.where(n == 0, 4, 0) + jnp.where((n == 1) | (n == 2), 2, 0)
     pl.semaphore_wait(barrier, targets)
 
     copies = []
@@ -215,22 +214,21 @@
     correction = finish - march(start_coarse[...])
     slots[n, pl.ds(6, 4)] = jnp.where(n == 0, finish, correction)
 
-    def term_copy(column):
-        return remote(
-            slots.at[n, pl.ds(6, 4)],
-            slots.at[n, pl.ds(6, 4)],
-            term_send.at[column],
-            term_recv.at[n],
-            {"cuts": seat(column, s)},
-        )
-
-    def wing_copy(m, source, target, width, step, side, send, column):
+    term_copy = remote(
+        slots.at[n, pl.ds(6, 4)],
+        slots.at[n, pl.ds(6, 4)],
+        term_send.at[0],
+        term_recv.at[n],
+        {"cuts": seat(s)},
+    )
+
+    def wing_copy(m, source, target, width, step, side, send):
         return remote(
             slots.at[m, pl.ds(6 + source, width)],
             slots.at[m, pl.ds(target, width)],
             send,
             wing_recv.at[m, side],
-            {"cuts": seat(column, at(step)), "space": at(step)},
+            {"cuts": seat(at(step)), "space": at(step)},
         )
 
     wings = (
@@ -240,14 +238,10 @@
     )
 
     def first_wings(m):
-        return [
-            wing_copy(m, *wing, first_send.at[column, wing[4]], column)
-            for column in range(4)
-            for wing in wings[m]
-        ]
+        return [wing_copy(m, *wing, first_send.at[wing[4]]) for wing in wings[m]]
 
     def later_wings(m, kind):
-        return [wing_copy(m, *wing, wing_send.at[m, wing[4]], x) for wing in wings[kind]]
+        return [wing_copy(m, *wing, wing_send.at[m, wing[4]]) for wing in wings[kind]]
 
     for m in range(3):
 
@@ -256,11 +250,9 @@
             for copy in first_wings(m):
                 copy.start()
 
-    for column in range(4):
-
-        @pl.when(n != seat(column, s))
-        def _():
-            term_copy(column).start()
+    @pl.when(jnp.logical_not(chain))
+    def _():
+        term_copy.start()
 
     def await_term(m):
         @pl.when(n != m)
@@ -274,13 +266,11 @@
         )
 
     def deliver(m, state):
-        @pl.when((lax.rem(m // 2, 4) == x) & (m > 0))
+        results[m] = state
+
+        @pl.when(m != n)
         def _():
-            results[m] = state
-
-            @pl.when(m != n)
-            def _():
-                result_copy(m).start()
+            result_copy(m).start()
 
     def wide_copies(r):
         return [
@@ -289,7 +279,7 @@
                 wides.at[r, pl.ds(target, 4)],
                 wide_send.at[r, side],
                 wide_recv.at[r, side],
-                {"cuts": seat(x, at(step)), "space": at(step)},
+                {"cuts": seat(at(step)), "space": at(step)},
             )
             for target, step, side in ((4, 1, 0), (12, -1, 1), (0, 2, 2), (16, -2, 3))
         ]
@@ -300,53 +290,58 @@
             for copy in later_wings(base + kind, kind):
                 copy.start()
 
-    def three_links(base, wide, r):
-        wide = march(wide) + slots[base + 1, 2:14]
+    def three_links(base, wide, r, arrive):
+        wide = march(wide)
+        arrive(1)
+        wide = wide + slots[base + 1, 2:14]
         deliver(base + 1, wide[4:8])
-        wide = march(wide) + slots[base + 2, 4:12]
+        wide = march(wide)
+        arrive(2)
+        wide = wide + slots[base + 2, 4:12]
         deliver(base + 2, wide[2:6])
-        state = march(wide) + slots[base + 3, 6:10]
+        wide = march(wide)
+        await_term(base + 3)
+        state = wide + slots[base + 3, 6:10]
         wides[r + 1, pl.ds(8, 4)] = state
 
         @pl.when(r < rounds - 1)
         def _():
             for copy in wide_copies(r + 1):
                 copy.start()
+            forward(base + 4)
 
         deliver(base + 3, state)
 
     @pl.when(chain)
     def _():
-        for m in range(4):
+        def arrive_first(m):
             await_term(m)
-        for m in range(3):
-            for copy in (wing_copy(m, *wing, first_send.at[0, wing[4]], x) for wing in wings[m]):
+            for copy in first_wings(m):
                 copy.wait_recv()
-        forward(4)
-        three_links(0, slots[0], 0)
+
+        arrive_first(0)
+        three_links(0, slots[0], 0, arrive_first)
 
         def one_round(r, carry):
             base = 4 * r
+
+            def arrive(kind):
+                for copy in later_wings(base + kind, kind):
+                    copy.wait()
+
             for copy in wide_copies(r):
                 copy.wait()
-            await_term(base + 3)
-            for kind in range(3):
-                for copy in later_wings(base + kind, kind):
-                    copy.wait()
-
-            @pl.when(r < rounds - 1)
-            def _():
-                forward(base + 4)
-
-            wide = march(wides[r]) + slots[base]
+            wide = march(wides[r])
+            arrive(0)
+            wide = wide + slots[base]
             deliver(base, wide[6:10])
-            three_links(base, wide, r)
+            three_links(base, wide, r, arrive)
             return carry
 
         lax.fori_loop(1, rounds, one_round, 0)
         for m in range(1, cuts):
 
-            @pl.when((m // 2 % 4 == x) & (m != n))
+            @pl.when(m != n)
             def _():
                 result_copy(m).wait_send()
 
@@ -385,11 +380,9 @@
             for copy in first_wings(m):
                 copy.wait_send()
 
-    for column in range(4):
-
-        @pl.when(n != seat(column, s))
-        def _():
-            term_copy(column).wait_send()
+    @pl.when(jnp.logical_not(chain))
+    def _():
+        term_copy.wait_send()
 
 
 def on_device(start_u, start_v):
@@ -423,9 +416,9 @@
             dma((2,)),
             dma((4,)),
             dma((4,)),
+            dma((1,)),
+            dma((cuts,)),
             dma((4,)),
-            dma((cuts,)),
-            dma((4, 4)),
             dma((cuts, 4)),
             dma((cuts, 4)),
             dma((rounds, 4)),

time: 62.4 us -> 57.9 us (0.928)
  the two profiles are of different devices: /device:TPU:6 before, /device:TPU:70 now
where the time goes in v3:
time: 57.9 us; the launch traced here: 57.4 us
  Pallas kernels  54.5 us (94%)
  local copies, waits for them, and re-layouts  2.26 us (4%)
  between operations  0.65 us (1%)
    pallas_call x1, Pallas kernels, on_device(): pl.pallas_call(body, out_shape=(shape, shape), in_specs=[hbm, hbm], out_s...  54.5 us
    unnamed x4, local copies, waits for them, and re-layouts  2.26 us

profile of v3, /device:TPU:70, one launch (start us, length us, event | category | flops | bytes accessed | tf_op | source)
XLA Modules:
  0.0 57.4 jit_solution(12323718779129038458)
XLA Ops:
  0.6 54.5 %parareal.1 = (f32[1,8,32,128]{3,2,1,0:T(8,128)}, f32[1,8,32,128]{3,2,1,0:T(8,128)}) custom-call(f32[1,8,32,128]{3,2,1,0:T(8,128)} %refs_0_.1, f32[1,8,32,128]{3,2,1,0:T(8,128)} %refs_1_.1), custom_call_target="tpu_custom_call" | custom-call | tf_op jit(solution)/shard_map/parareal/pallas_call | solution.py:402
  55.1 0.0 copy-start
  55.2 1.6 %copy.6 = f32[1,8,32,128]{3,2,1,0:T(8,128)} copy(f32[1,8,32,128]{3,2,1,0:T(8,128)} %get-tuple-element.4) | data formatting | bytes 262144
  56.8 0.0 copy-done
  56.8 0.7 %copy.7 = f32[1,8,32,128]{3,2,1,0:T(8,128)} copy(f32[1,8,32,128]{3,2,1,0:T(8,128)S(1)} %copy-done) | data formatting | bytes 262144
Async XLA Ops:
  55.1 1.6 %copy-start = (f32[1,8,32,128]{3,2,1,0:T(8,128)S(1)}, f32[1,8,32,128]{3,2,1,0:T(8,128)}, u32[]{:S(2)}) copy-start(f32[1,8,32,128]{3,2,1,0:T(8,128)} %get-tuple-element.5) | copy-start | bytes 393220

commit v4 on v3

--- a/solution.py
+++ b/solution.py
@@ -93,8 +93,8 @@
     space,
     u_ref,
     v_ref,
-    out_u,
-    out_v,
+    finals,
+    change_ref,
     fine,
     rows,
     start_coarse,
@@ -106,6 +106,7 @@
     load_sem,
     fine_send,
     fine_recv,
+    turn,
     term_send,
     term_recv,
     first_send,
@@ -119,6 +120,10 @@
     n = lax.axis_index("cuts")
     s = lax.axis_index("space")
     rounds = cuts // 4
+    half = cuts // 2
+    upper = n >= half
+    row = lax.rem(s, 8)
+    edge = (row == 7, row == 0)
 
     def at(step):
         return lax.rem(s + step + space, space)
@@ -159,6 +164,10 @@
     def _():
         greet({"cuts": seat(s)})
 
+    @pl.when(upper & (edge[0] | edge[1]))
+    def _():
+        greet({"cuts": n - half})
+
     now = fine.at[0]
     loads = []
     for k, ref in enumerate((u_ref, v_ref)):
@@ -169,6 +178,7 @@
         load.start()
 
     targets = 2 + jnp.where(chain, 4 + cuts - 1, 1)
+    targets = targets + jnp.where(jnp.logical_not(upper) & (edge[0] | edge[1]), 1, 0)
     targets = targets + jnp.where(n == 0, 4, 0) + jnp.where((n == 1) | (n == 2), 2, 0)
     pl.semaphore_wait(barrier, targets)
 
@@ -192,16 +202,39 @@
                 {"space": at(-1)},
             )
         )
-    for copy in copies:
-        copy.start()
+    def start(which):
+        for copy in copies[which::2]:
+            copy.start()
+
+    for which in range(2):
+
+        @pl.when(jnp.logical_not(upper & edge[which]))
+        def _():
+            start(which)
+
     for load in loads:
         load.wait()
 
     restrict(now, HALO, rows, start_coarse, 2, COARSE)
     for t in range(3):
         fine_planes(fine.at[t % 2], fine.at[(t + 1) % 2], HALO + 1 + t, PLANES - 2 - 2 * t)
+    for which in range(2):
+
+        @pl.when(upper & edge[which])
+        def _():
+            pl.semaphore_wait(turn, 1)
+            start(which)
+
+        @pl.when(jnp.logical_not(upper) & edge[which])
+        def _():
+            for copy in copies[which::2]:
+                copy.wait_send()
+            pl.semaphore_signal(
+                turn, inc=1, device_id={"cuts": n + half}, device_id_type=MESH
+            )
+
     for copy in copies:
-        copy.wait()
+        copy.wait_recv()
     restrict(now, 0, rows, start_coarse, 0, 2)
     restrict(now, HALO + PLANES, rows, start_coarse, COARSE + 2, 2)
     for t in range(3):
@@ -209,6 +242,10 @@
         fine_planes(source, target, t + 1, HALO)
         fine_planes(source, target, PADDED - 1 - HALO - t, HALO)
     fine_planes(fine.at[1], fine.at[0], HALO, PLANES)
+    outs = [
+        pltpu.make_async_copy(now.at[k, pl.ds(HALO, PLANES)], finals.at[k], load_sem.at[k])
+        for k in range(2)
+    ]
     restrict(now, HALO, rows, end_coarse, 0, COARSE)
     finish = end_coarse[...]
     correction = finish - march(start_coarse[...])
@@ -253,6 +290,9 @@
     @pl.when(jnp.logical_not(chain))
     def _():
         term_copy.start()
+
+    for out in outs:
+        out.start()
 
     def await_term(m):
         @pl.when(n != m)
@@ -357,7 +397,31 @@
     def _():
         result_copy(n).wait_recv()
 
-    change = mine[...] - end_coarse[...]
+    change_ref[...] = mine[...] - end_coarse[...]
+    for out in outs:
+        out.wait()
+
+    for m in range(3):
+
+        @pl.when(n == m)
+        def _():
+            for copy in first_wings(m):
+                copy.wait_send()
+
+    @pl.when(jnp.logical_not(chain))
+    def _():
+        term_copy.wait_send()
+
+    for which in range(2):
+
+        @pl.when(upper | jnp.logical_not(edge[which]))
+        def _():
+            for copy in copies[which::2]:
+                copy.wait_send()
+
+
+def finish_kernel(finals, change_ref, out_u, out_v, rows):
+    change = change_ref[...]
     even = even_lanes(change.shape)
     for k, (out, spread) in enumerate(
         (
@@ -370,19 +434,8 @@
             rows[slot, pl.ds(0, CY, stride=2)] = spread[i]
             rows[slot, pl.ds(1, CY, stride=2)] = spread[i]
             added = rows[slot]
-            out[0, 2 * i] = fine[0, k, HALO + 2 * i] + added
-            out[0, 2 * i + 1] = fine[0, k, HALO + 2 * i + 1] + added
-
-    for m in range(3):
-
-        @pl.when(n == m)
-        def _():
-            for copy in first_wings(m):
-                copy.wait_send()
-
-    @pl.when(jnp.logical_not(chain))
-    def _():
-        term_copy.wait_send()
+            out[0, 2 * i] = finals[k, 2 * i] + added
+            out[0, 2 * i + 1] = finals[k, 2 * i + 1] + added
 
 
 def on_device(start_u, start_v):
@@ -399,11 +452,14 @@
     def body(*refs):
         kernel(cuts, space, *refs)
 
-    return pl.pallas_call(
+    finals, change = pl.pallas_call(
         body,
-        out_shape=(shape, shape),
+        out_shape=(
+            jax.ShapeDtypeStruct((2, PLANES, GY, GZ), f32),
+            jax.ShapeDtypeStruct(block, f32),
+        ),
         in_specs=[hbm, hbm],
-        out_specs=(vmem, vmem),
+        out_specs=(hbm, vmem),
         scratch_shapes=[
             pltpu.VMEM((2, 2, PADDED, GY, GZ), f32),
             pltpu.VMEM((PADDED // 2, GY, GZ), f32),
@@ -416,6 +472,7 @@
             dma((2,)),
             dma((4,)),
             dma((4,)),
+            pltpu.SemaphoreType.REGULAR,
             dma((1,)),
             dma((cuts,)),
             dma((4,)),
@@ -429,6 +486,14 @@
         compiler_params=pltpu.CompilerParams(collective_id=0, has_side_effects=True),
         name="parareal",
     )(start_u, start_v)
+    return pl.pallas_call(
+        finish_kernel,
+        out_shape=(shape, shape),
+        in_specs=[vmem, vmem],
+        out_specs=(vmem, vmem),
+        scratch_shapes=[pltpu.VMEM((2 * COARSE, GY, GZ), f32)],
+        name="finish",
+    )(finals, change)
 
 
 def solution(mesh):

time: 57.9 us -> 56.4 us (0.974)
  local copies, waits for them, and re-layouts: 2.26 us -> 0 us
  Pallas kernels: 54.5 us -> 55.3 us
    unnamed x4 -> x0, local copies, waits for them, and re-layouts: 2.26 us -> none
    pallas_call x1 -> x2, Pallas kernels: 54.5 us -> 55.3 us  [the longest x1 53.5 us: on_device(): pl.pallas_call(body, out_shape=(jax.ShapeDtypeStruct((2, PLANES, GY, GZ),...]
where the time goes in v4:
time: 56.4 us; the launch traced here: 55.9 us
  Pallas kernels  55.3 us (98%)
  between operations  0.64 us (1%)
    pallas_call x1, Pallas kernels, on_device(): pl.pallas_call(body, out_shape=(jax.ShapeDtypeStruct((2, PLANES, GY, GZ),...  53.5 us
    pallas_call x1, Pallas kernels, on_device(): pl.pallas_call(finish_kernel, out_shape=(shape, shape), in_specs=[vmem, v...  1.74 us

profile of v4, /device:TPU:70, one launch (start us, length us, event | category | flops | bytes accessed | tf_op | source)
XLA Modules:
  0.0 55.9 jit_solution(3416646074623037297)
XLA Ops:
  0.6 53.5 %parareal.1 = (f32[2,8,32,128]{3,2,1,0:T(8,128)}, f32[4,16,128]{2,1,0:T(8,128)}) custom-call(f32[1,8,32,128]{3,2,1,0:T(8,128)} %refs_0_.1, f32[1,8,32,128]{3,2,1,0:T(8,128)} %refs_1_.1), custom_call_target="tpu_custom_call" | custom-call | tf_op jit(solution)/shard_map/parareal/pallas_call | solution.py:455
  54.2 1.7 %finish.1 = (f32[1,8,32,128]{3,2,1,0:T(8,128)}, f32[1,8,32,128]{3,2,1,0:T(8,128)}) custom-call(f32[2,8,32,128]{3,2,1,0:T(8,128)} %get-tuple-element.4.finals, f32[4,16,128]{2,1,0:T(8,128)} %get-tuple-element.5.change_ref), custom_call_target="tpu_custom_call" | custom-call | tf_op jit(solution)/shard_map/finish/pallas_call | solution.py:489

commit v5 on v4

--- a/solution.py
+++ b/solution.py
@@ -269,7 +269,7 @@
         )
 
     wings = (
-        ((0, 2, 4, 1, 0), (0, 10, 4, -1, 1), (2, 0, 2, 2, 2), (0, 14, 2, -2, 3)),
+        ((2, 0, 2, 2, 2), (0, 14, 2, -2, 3), (0, 2, 4, 1, 0), (0, 10, 4, -1, 1)),
         ((0, 2, 4, 1, 0), (0, 10, 4, -1, 1)),
         ((2, 4, 2, 1, 0), (0, 10, 2, -1, 1)),
     )
@@ -321,7 +321,7 @@
                 wide_recv.at[r, side],
                 {"cuts": seat(at(step)), "space": at(step)},
             )
-            for target, step, side in ((4, 1, 0), (12, -1, 1), (0, 2, 2), (16, -2, 3))
+            for target, step, side in ((0, 2, 2), (16, -2, 3), (4, 1, 0), (12, -1, 1))
         ]
 
     def forward(base):

time: 56.4 us -> 55.9 us (level)
  no operation moved by 1% of the time
where the time goes in v5:
time: 55.9 us; the launch traced here: 55.4 us
  Pallas kernels  54.8 us (98%)
  between operations  0.64 us (1%)
    pallas_call x1, Pallas kernels, on_device(): pl.pallas_call(body, out_shape=(jax.ShapeDtypeStruct((2, PLANES, GY, GZ),...  53 us
    pallas_call x1, Pallas kernels, on_device(): pl.pallas_call(finish_kernel, out_shape=(shape, shape), in_specs=[vmem, v...  1.74 us

profile of v5, /device:TPU:70, one launch (start us, length us, event | category | flops | bytes accessed | tf_op | source)
XLA Modules:
  0.0 55.4 jit_solution(13252901464510977506)
XLA Ops:
  0.6 53.0 %parareal.1 = (f32[2,8,32,128]{3,2,1,0:T(8,128)}, f32[4,16,128]{2,1,0:T(8,128)}) custom-call(f32[1,8,32,128]{3,2,1,0:T(8,128)} %refs_0_.1, f32[1,8,32,128]{3,2,1,0:T(8,128)} %refs_1_.1), custom_call_target="tpu_custom_call" | custom-call | tf_op jit(solution)/shard_map/parareal/pallas_call | solution.py:455
  53.7 1.7 %finish.1 = (f32[1,8,32,128]{3,2,1,0:T(8,128)}, f32[1,8,32,128]{3,2,1,0:T(8,128)}) custom-call(f32[2,8,32,128]{3,2,1,0:T(8,128)} %get-tuple-element.4.finals, f32[4,16,128]{2,1,0:T(8,128)} %get-tuple-element.5.change_ref), custom_call_target="tpu_custom_call" | custom-call | tf_op jit(solution)/shard_map/finish/pallas_call | solution.py:489

commit v6 on v5

--- a/solution.py
+++ b/solution.py
@@ -70,7 +70,7 @@
         )
         return carry
 
-    lax.fori_loop(0, count, body, 0, unroll=2)
+    lax.fori_loop(0, count, body, 0, unroll=2 if count % 4 else 4)
 
 
 def restrict(source, first, rows, out, place, count):
@@ -85,7 +85,7 @@
         )
         return carry
 
-    lax.fori_loop(0, count, body, 0)
+    lax.fori_loop(0, count, body, 0, unroll=2)
 
 
 def kernel(

time: 55.9 us -> 54.6 us (0.977)
  Pallas kernels: 54.8 us -> 53.5 us
    pallas_call x1, Pallas kernels: 53 us -> 51.7 us  [on_device(): pl.pallas_call(body, out_shape=(jax.ShapeDtypeStruct((2, PLANES, GY, GZ),...]
where the time goes in v6:
time: 54.6 us; the launch traced here: 54.1 us
  Pallas kernels  53.5 us (98%)
  between operations  0.64 us (1%)
    pallas_call x1, Pallas kernels, on_device(): pl.pallas_call(body, out_shape=(jax.ShapeDtypeStruct((2, PLANES, GY, GZ),...  51.7 us
    pallas_call x1, Pallas kernels, on_device(): pl.pallas_call(finish_kernel, out_shape=(shape, shape), in_specs=[vmem, v...  1.74 us

profile of v6, /device:TPU:70, one launch (start us, length us, event | category | flops | bytes accessed | tf_op | source)
XLA Modules:
  0.0 54.1 jit_solution(3968981224695988493)
XLA Ops:
  0.6 51.7 %parareal.1 = (f32[2,8,32,128]{3,2,1,0:T(8,128)}, f32[4,16,128]{2,1,0:T(8,128)}) custom-call(f32[1,8,32,128]{3,2,1,0:T(8,128)} %refs_0_.1, f32[1,8,32,128]{3,2,1,0:T(8,128)} %refs_1_.1), custom_call_target="tpu_custom_call" | custom-call | tf_op jit(solution)/shard_map/parareal/pallas_call | solution.py:455
  52.4 1.7 %finish.1 = (f32[1,8,32,128]{3,2,1,0:T(8,128)}, f32[1,8,32,128]{3,2,1,0:T(8,128)}) custom-call(f32[2,8,32,128]{3,2,1,0:T(8,128)} %get-tuple-element.4.finals, f32[4,16,128]{2,1,0:T(8,128)} %get-tuple-element.5.change_ref), custom_call_target="tpu_custom_call" | custom-call | tf_op jit(solution)/shard_map/finish/pallas_call | solution.py:489

commit v7 on v6

--- a/solution.py
+++ b/solution.py
@@ -70,7 +70,7 @@
         )
         return carry
 
-    lax.fori_loop(0, count, body, 0, unroll=2 if count % 4 else 4)
+    lax.fori_loop(0, count, body, 0, unroll=count)
 
 
 def restrict(source, first, rows, out, place, count):
@@ -85,7 +85,7 @@
         )
         return carry
 
-    lax.fori_loop(0, count, body, 0, unroll=2)
+    lax.fori_loop(0, count, body, 0, unroll=count)
 
 
 def kernel(

time: 54.6 us -> 54.3 us (level)
  no operation moved by 1% of the time
where the time goes in v7:
time: 54.3 us; the launch traced here: 53.8 us
  Pallas kernels  53.2 us (98%)
  between operations  0.64 us (1%)
    pallas_call x1, Pallas kernels, on_device(): pl.pallas_call(body, out_shape=(jax.ShapeDtypeStruct((2, PLANES, GY, GZ),...  51.4 us
    pallas_call x1, Pallas kernels, on_device(): pl.pallas_call(finish_kernel, out_shape=(shape, shape), in_specs=[vmem, v...  1.74 us

profile of v7, /device:TPU:70, one launch (start us, length us, event | category | flops | bytes accessed | tf_op | source)
XLA Modules:
  0.0 53.8 jit_solution(8662877701238217822)
XLA Ops:
  0.6 51.4 %parareal.1 = (f32[2,8,32,128]{3,2,1,0:T(8,128)}, f32[4,16,128]{2,1,0:T(8,128)}) custom-call(f32[1,8,32,128]{3,2,1,0:T(8,128)} %refs_0_.1, f32[1,8,32,128]{3,2,1,0:T(8,128)} %refs_1_.1), custom_call_target="tpu_custom_call" | custom-call | tf_op jit(solution)/shard_map/parareal/pallas_call | solution.py:455
  52.0 1.7 %finish.1 = (f32[1,8,32,128]{3,2,1,0:T(8,128)}, f32[1,8,32,128]{3,2,1,0:T(8,128)}) custom-call(f32[2,8,32,128]{3,2,1,0:T(8,128)} %get-tuple-element.4.finals, f32[4,16,128]{2,1,0:T(8,128)} %get-tuple-element.5.change_ref), custom_call_target="tpu_custom_call" | custom-call | tf_op jit(solution)/shard_map/finish/pallas_call | solution.py:489
